TPU v7x, 256 devices: a whole 4x4x8 slice. The times are simulated.
256 devices in a mesh: row: 16 (over x, y), col: 16 (over z, core).
Axes of the slice: x: 4, y: 4, z: 8, core: 2. Of those that a mesh axis runs over, the one named last changes fastest.
Arguments:
- target: float32 [8, 16, 128, 8, 16, 128], P(None, 'row', None, None, 'col'), may hold values from -6 to 6
- panel_a: bfloat16 [2, 32, 128, 512], P(None, 'col'), may hold values from -1.1953125 to 1.1953125
- inv_factor: bfloat16 [2, 512, 512], replicated, as said below
- panel_rhs: bfloat16 [2, 512, 256], P(None, 'col'), may hold values from -6 to 6
- panel_rows: int32 [2, 32], replicated, may hold values from 0 to 127, as said below
- right_sides: float32 [8, 16, 128, 256], P(None, 'col'), may hold values from -12 to 12
Outputs:
- updated_target: float32 [8, 16, 128, 8, 16, 128], P(None, 'row', None, None, 'col')
- updated_sides: float32 [8, 16, 128, 256], P(None, 'col')
Inputs may be any that keep to these rules, and one draw needn't show every extreme that they name: `panel_rows`: each row holds 32 distinct positions in increasing order, the first 0 and the last 127. `inv_factor`: lower triangular, diagonal between 0.5 and 2.
All inputs are finite; a program needn't handle non-finite values.
Results may differ from a plain program's by a relative error of at most 0.0035.
Values may be sent and summed in bfloat16 or wider, within the bound.
A program may use at most 128 MiB of HBM per device.

v0:
```python
import jax
import jax.numpy as jnp
from jax import lax
from jax.sharding import PartitionSpec as P


def shards(target, panel_a, inv_factor, panel_rhs, panel_rows, right_sides):
    row_count = lax.axis_size("row")
    col_count = lax.axis_size("col")
    row_index = lax.axis_index("row")
    col_index = lax.axis_index("col")
    tile_rows = target.shape[2]
    row_blocks = target.shape[0]
    col_blocks = target.shape[3]
    slab_rows = tile_rows // row_count
    shard_rows = panel_rhs.shape[1]
    updated_target = target
    updated_sides = right_sides
    row_places = jnp.arange(row_blocks, dtype=jnp.int32) * row_count + row_index
    col_places = jnp.arange(col_blocks, dtype=jnp.int32) * col_count + col_index
    for which_panel in range(2):
        factor = inv_factor[which_panel]
        positions = panel_rows[which_panel]
        own_rows = lax.dynamic_slice_in_dim(
            panel_a[which_panel], row_index * slab_rows, slab_rows, 1
        )
        solved_piece = jnp.einsum(
            "axq,pq->axp", own_rows, factor, preferred_element_type=jnp.float32
        ).astype(jnp.bfloat16)
        column_tiles = lax.all_gather(solved_piece, "row", axis=1, tiled=True)
        all_tiles = lax.all_gather(column_tiles, "col", axis=0, tiled=True)
        columns = lax.dynamic_slice_in_dim(factor, col_index * shard_rows, shard_rows, 1)
        local_term = jnp.dot(columns, panel_rhs[which_panel], preferred_element_type=jnp.float32)
        partial_value = lax.psum(local_term, "col").astype(jnp.bfloat16)
        pick_rows = (positions[None, :] == row_places[:, None]).astype(jnp.bfloat16)
        pick_cols = (positions[None, :] == col_places[:, None]).astype(jnp.bfloat16)
        row_set = jnp.einsum(
            "ia,axp->ixp", pick_rows, all_tiles, preferred_element_type=jnp.float32
        ).astype(jnp.bfloat16)
        col_set = jnp.einsum(
            "ka,axp->kxp", pick_cols, all_tiles, preferred_element_type=jnp.float32
        ).astype(jnp.bfloat16)
        schur_term = jnp.einsum(
            "ixp,kyp->ixky", row_set, col_set, preferred_element_type=jnp.float32
        )
        updated_target = updated_target - schur_term[:, None, :, :, None, :]
        side_term = jnp.einsum(
            "kxp,pn->kxn", col_set, partial_value, preferred_element_type=jnp.float32
        )
        updated_sides = updated_sides - side_term[:, None]
    return (updated_target, updated_sides)


def solution(mesh):
    placed = (
        P(None, "row", None, None, "col", None),
        P(None, "col", None, None),
        P(),
        P(None, "col", None),
        P(),
        P(None, "col", None, None),
    )
    return jax.shard_map(
        shards,
        mesh=mesh,
        in_specs=placed,
        out_specs=(P(None, "row", None, None, "col", None), P(None, "col", None, None)),
        check_vma=False,
    )
```

profile of v0, /device:TPU:1, one launch (start us, length us, event | category | flops | bytes accessed | tf_op | source)
XLA Modules:
  0.0 167.5 jit_solution(11555292527745360764)
XLA Ops:
  7.2 0.0 all-gather.5.cloned.1.call-start
  7.2 1.1 fusion.73
  8.3 1.3 convolution_convert_fusion
  9.6 21.6 %all_gather.14 = bf16[2,128,512]{2,1,0:T(8,128)(2,1)} all-gather(bf16[2,8,512]{2,1,0:T(8,128)(2,1)S(1)} %convolution_convert_fusion), channel_id=1, replica_groups=mesh['row'=16,'col'=16] {'row'}, dimensions={1}, use_global_device_ids=true | all-gather | bytes 278528 | tf_op jit(solution)/shard_map/all_gather | solution.py:30
  31.2 0.0 all-gather.5.cloned.1.call-update
  31.2 0.0 all-gather.3.cloned.1.call-start
  31.3 1.3 convolution_convert_fusion.1
  32.5 19.2 %all_gather.12 = bf16[2,128,512]{2,1,0:T(8,128)(2,1)} all-gather(bf16[2,8,512]{2,1,0:T(8,128)(2,1)S(1)} %convolution_convert_fusion.1), channel_id=1, replica_groups=mesh['row'=16,'col'=16] {'row'}, dimensions={1}, use_global_device_ids=true | all-gather | bytes 278528 | tf_op jit(solution)/shard_map/all_gather | solution.py:30
  51.7 0.0 all-gather.3.cloned.1.call-update
  51.8 1.3 fusion.72
  53.0 0.3 fusion.34
  53.3 0.3 fusion.36
  53.7 77.4 %all-reduce.2 = (bf16[512,256]{1,0:T(8,128)(2,1)S(1)}, bf16[512,256]{1,0:T(8,128)(2,1)S(1)}) all-reduce(f32[512,256]{1,0:T(8,128)S(1)} %fusion.34, f32[512,256]{1,0:T(8,128)S(1)} %fusion.36), channel_id=1, replica_groups=mesh['row'=16,'col'=16] {'col'}, use_global_device_ids=true, to_apply=%region_1.0 | all-reduce | flops 262144 | bytes 1572864 | tf_op jit(solution)/shard_map/psum | solution.py:34
  131.1 0.0 all-gather.5.cloned.1.call-done
  131.1 4.5 %fusion.11 = bf16[8,128,512]{2,0,1:T(8,128)(2,1)S(1)} fusion(bf16[32,128,512]{2,1,0:T(8,128)(2,1)} %all-gather.5.cloned.1.call-done, s32[32]{0:T(128)S(1)} %get-tuple-element.12, s32[8]{0:T(128)S(1)} %fusion.68), kind=kOutput, calls=%fused_computation.13 | convolution fusion | flops 34078976 | bytes 5243040 | tf_op jit(solution)/shard_map/ka,axp->kxp/dot_general | solution.py:40
  135.6 1.7 %convolution_bitcast_fusion = f32[8,1,128,256]{3,2,0,1:T(8,128)} fusion(bf16[8,128,512]{2,0,1:T(8,128)(2,1)S(1)} %fusion.11, bf16[512,256]{1,0:T(8,128)(2,1)S(1)} %get-tuple-element.6), kind=kOutput, calls=%fused_computation.14 | convolution fusion | flops 268435456 | bytes 2359296 | tf_op jit(solution)/shard_map/kxp,pn->kxn/dot_general | solution.py:47
  137.3 4.7 %fusion.8 = bf16[8,128,512]{2,0,1:T(8,128)(2,1)S(1)} fusion(bf16[32,128,512]{2,1,0:T(8,128)(2,1)} %all-gather.3.cloned.1.call-done, s32[32]{0:T(128)S(1)} %get-tuple-element.13, s32[8]{0:T(128)S(1)} %fusion.68), kind=kOutput, calls=%fused_computation.12 | convolution fusion | flops 34078976 | bytes 5243040 | tf_op jit(solution)/shard_map/ka,axp->kxp/dot_general | solution.py:40
  142.1 2.4 %fusion.4 = bf16[8,128,512]{2,0,1:T(8,128)(2,1)S(1)} fusion(bf16[32,128,512]{2,1,0:T(8,128)(2,1)S(1)} %copy-done.1, s32[32]{0:T(128)S(1)} %get-tuple-element.13, s32[8]{0:T(128)S(1)} %fusion.69), kind=kOutput, calls=%fused_computation.6 | convolution fusion | flops 33554688 | bytes 5243040 | tf_op jit(solution)/shard_map/ia,axp->ixp/dot_general | solution.py:37
  144.4 1.7 fusion.18
  146.1 0.5 copy-done
  146.6 2.4 %fusion = bf16[8,128,512]{2,0,1:T(8,128)(2,1)S(1)} fusion(bf16[32,128,512]{2,1,0:T(8,128)(2,1)S(1)} %copy-done, s32[32]{0:T(128)S(1)} %get-tuple-element.12, s32[8]{0:T(128)S(1)} %fusion.69), kind=kOutput, calls=%fused_computation.2 | convolution fusion | flops 33554688 | bytes 5243040 | tf_op jit(solution)/shard_map/ia,axp->ixp/dot_general | solution.py:37
  149.0 2.4 %bitcast_subtract_fusion = f32[8,1,128,8,1,128]{5,2,3,0,4,1:T(8,128)S(1)} fusion(f32[8,128,8,128]{3,1,2,0:T(8,128)S(1)} %fusion.18, f32[8,1,128,8,1,128]{5,4,3,2,1,0:T(1,128)S(1)} %copy-done.2, bf16[8,128,512]{2,0,1:T(8,128)(2,1)S(1)} %fusion, bf16[8,128,512]{2,0,1:T(8,128)(2,1)S(1)} %fusion.11), kind=kOutput, calls=%fused_computation | convolution fusion | flops 1075838976 | bytes 14680064 | tf_op jit(solution)/shard_map/ixp,kyp->ixky/dot_general | solution.py:43
  151.4 6.3 %copy.26 = f32[8,1,128,8,1,128]{5,4,3,2,1,0:T(1,128)} copy(f32[8,1,128,8,1,128]{5,2,3,0,4,1:T(8,128)S(1)} %bitcast_subtract_fusion) | data formatting | bytes 8388608
  157.7 2.9 %fusion.16 = f32[8,1,128,256]{3,2,1,0:T(8,128)} fusion(f32[8,1,128,256]{3,2,0,1:T(8,128)S(1)} %copy-done.3, f32[8,1,128,256]{3,2,1,0:T(8,128)} %param.11, bf16[8,128,512]{2,0,1:T(8,128)(2,1)S(1)} %fusion.8, bf16[512,256]{1,0:T(8,128)(2,1)S(1)} %get-tuple-element.7), kind=kOutput, calls=%fused_computation.18 | convolution fusion | flops 268959744 | bytes 4456448 | tf_op jit(solution)/shard_map/kxp,pn->kxn/dot_general | solution.py:47
  (15 shorter events, 0.0 us)
Async XLA Ops:
  7.2 45.9 %copy-start.4 = (bf16[2,32,256]{2,1,0:T(8,128)(2,1)S(1)}, bf16[2,32,256]{2,1,0:T(8,128)(2,1)}, u32[]{:S(2)}) copy-start(bf16[2,32,256]{2,1,0:T(8,128)(2,1)} %param.9) | copy-start | bytes 98308
  7.2 46.5 %copy-start.5 = (s32[2,32]{1,0:T(2,128)S(1)}, s32[2,32]{1,0:T(2,128)}, u32[]{:S(2)}) copy-start(s32[2,32]{1,0:T(2,128)} %param.10) | copy-start | bytes 772
  7.2 123.9 %all-gather.5.cloned.1.call-start = ((), (), s32[]{:S(2)}) async-start(), calls=%async_computation.1 | async-start | bytes 4456448 | tf_op jit(solution)/shard_map/all_gather | solution.py:31
  31.2 106.1 %all-gather.3.cloned.1.call-start = ((), (), s32[]{:S(2)}) async-start(), calls=%async_computation | async-start | bytes 4456448 | tf_op jit(solution)/shard_map/all_gather | solution.py:31
  137.3 4.7 %copy-start.1 = (bf16[32,128,512]{2,1,0:T(8,128)(2,1)S(1)}, bf16[32,128,512]{2,1,0:T(8,128)(2,1)}, u32[]{:S(2)}) copy-start(bf16[32,128,512]{2,1,0:T(8,128)(2,1)} %all-gather.3.cloned.1.call-done) | copy-start | bytes 12582916
  144.4 2.2 %copy-start = (bf16[32,128,512]{2,1,0:T(8,128)(2,1)S(1)}, bf16[32,128,512]{2,1,0:T(8,128)(2,1)}, u32[]{:S(2)}) copy-start(bf16[32,128,512]{2,1,0:T(8,128)(2,1)} %all-gather.5.cloned.1.call-done) | copy-start | bytes 12582916
  146.6 2.4 %copy-start.2 = (f32[8,1,128,8,1,128]{5,4,3,2,1,0:T(1,128)S(1)}, f32[8,1,128,8,1,128]{5,4,3,2,1,0:T(1,128)}, u32[]{:S(2)}) copy-start(f32[8,1,128,8,1,128]{5,4,3,2,1,0:T(1,128)} %param.6) | copy-start | bytes 12582916
  151.3 6.3 %copy-start.3 = (f32[8,1,128,256]{3,2,0,1:T(8,128)S(1)}, f32[8,1,128,256]{3,2,0,1:T(8,128)}, u32[]{:S(2)}) copy-start(f32[8,1,128,256]{3,2,0,1:T(8,128)} %convolution_bitcast_fusion) | copy-start | bytes 3145732
Sparse Core Ops, SparseCore 0:
  31.3 49.0 all-gather.4
  82.2 43.1 all-gather.2
where the time goes:
time: 168 us; the launch traced here: 167 us
  blocking collectives  118 us (70%)
  matrix products  25.8 us (15%)
  between operations  14.2 us (8%)
  local copies, waits for them, and re-layouts  9.21 us (5%)
    psum x1, blocking collectives, shards(): partial_value = lax.psum(local_term, 'col').astype(jnp.bfloat16)  77.4 us
    all_gather x2, blocking collectives, shards(): column_tiles = lax.all_gather(solved_piece, 'row', axis=1, tiled=True)  40.8 us
    dot_general x2, matrix products, shards(): jnp.einsum('ka,axp->kxp', pick_cols, all_tiles, preferred_element_type=jn...  9.25 us
    unnamed x13, local copies, waits for them, and re-layouts  6.87 us
    dot_general x2, matrix products, shards(): jnp.einsum('ia,axp->ixp', pick_rows, all_tiles, preferred_element_type=jn...  4.72 us
    dot_general x2, matrix products, shards(): jnp.einsum('kxp,pn->kxn', col_set, partial_value, preferred_element_type=...  4.65 us
    dot_general x2, matrix products, shards(): jnp.einsum('ixp,kyp->ixky', row_set, col_set, preferred_element_type=jnp....  4.02 us
  transfers between devices with their start and end apart: 2, of which 0 were waited for; matrix products, arithmetic and copies ran while one was open for 6% of the time, Pallas kernels for 0%

commit v1 on v0

v1 whole, which is shorter than its diff:
```python
import functools

import jax
import jax.numpy as jnp
from jax import lax
from jax.experimental import pallas as pl
from jax.experimental.pallas import tpu as pltpu
from jax.sharding import PartitionSpec as P

MESH = pl.DeviceIdType.MESH
NX, NY, NZ = 4, 4, 8
NROW, NCOL = 16, 16
SLOTS = 16
SLAB = 8
PW = 512
ZERO_BLOCK = 64


class Copies:
    def __init__(self):
        self.sent = []

    def start(self, src, dst, send_sem, recv_sem, device):
        copy = pltpu.make_async_remote_copy(
            src_ref=src,
            dst_ref=dst,
            send_sem=send_sem,
            recv_sem=recv_sem,
            device_id=device,
            device_id_type=MESH,
        )
        copy.start()
        self.sent.append(copy)

    def arrived(self, ref, send_sem, recv_sem, device):
        pltpu.make_async_remote_copy(
            src_ref=ref,
            dst_ref=ref,
            send_sem=send_sem,
            recv_sem=recv_sem,
            device_id=device,
            device_id_type=MESH,
        ).wait_recv()

    def finish(self):
        for copy in self.sent:
            copy.wait_send()


class ZRing:
    def __init__(self, copies, whole, half, place, send, recv, mate_send, mate_recv):
        self.copies, self.whole, self.half = copies, whole, half
        self.row, self.z, self.k = place
        self.send, self.recv = send, recv
        self.mate_send, self.mate_recv = mate_send, mate_recv

    def chip(self, distance):
        return lax.rem(self.z + distance + NZ, NZ)

    def device(self, distance):
        return (self.row, self.chip(distance) * 2 + self.k)

    def piece(self, core, way, hops):
        origin = self.chip(-hops if way == 0 else hops) * 2 + core
        return self.half(origin, way) if hops == NZ // 2 else self.whole(origin)

    def to_mate(self, way, hops):
        ref = self.piece(self.k, way, hops)
        at = way * 4 + hops
        self.copies.start(
            ref, ref, self.mate_send.at[at], self.mate_recv.at[at], (self.row, self.z * 2 + 1 - self.k)
        )

    def pass_on(self, way, hops):
        origin = self.chip(-hops if way == 0 else hops) * 2 + self.k
        ref = self.half(origin, way) if hops + 1 == NZ // 2 else self.whole(origin)
        self.copies.start(
            ref, ref, self.send.at[way, hops], self.recv.at[way, hops], self.device(1 if way == 0 else -1)
        )

    def begin(self):
        for way in range(2):
            self.pass_on(way, 0)
        self.to_mate(0, 0)

    def step(self, hops):
        for way in range(2):
            ref = self.piece(self.k, way, hops)
            self.copies.arrived(
                ref, self.send.at[way, hops - 1], self.recv.at[way, hops - 1], self.device(1 if way == 0 else -1)
            )
            if hops < NZ // 2:
                self.pass_on(way, hops)
            self.to_mate(way, hops)

    def end(self):
        mate = (self.row, self.z * 2 + 1 - self.k)
        for way in range(2):
            for hops in range(way, NZ // 2 + 1):
                ref = self.piece(1 - self.k, way, hops)
                at = way * 4 + hops
                self.copies.arrived(ref, self.mate_send.at[at], self.mate_recv.at[at], mate)


class PlaneGather:
    def __init__(self, copies, cols, half, place, send1, recv1, send2, recv2):
        self.copies, self.cols, self.half = copies, cols, half
        self.x, self.y, self.col = place
        self.send1, self.recv1, self.send2, self.recv2 = send1, recv1, send2, recv2

    def row(self, along, across):
        dx, dy = (along, across) if self.half == 0 else (across, along)
        return lax.rem(self.x + dx + NX, NX) * NY + lax.rem(self.y + dy + NY, NY)

    def device(self, along, across):
        return (self.row(along, across), self.col)

    def ref(self, along, across, part):
        start = self.half * 8 + (0 if part is None else part * 4)
        return self.cols.at[self.row(along, across), pl.ds(start, 8 if part is None else 4)]

    def shift(self, item):
        return (0, -1, 1, 2, 2)[item]

    def part(self, item):
        return (None, None, None, 0, 1)[item]

    def across_send(self, item):
        for way in range(2):
            ref = self.ref(self.shift(item), 0, self.part(item))
            self.copies.start(
                ref,
                ref,
                self.send2.at[item, way, 0],
                self.recv2.at[item, way, 0],
                self.device(0, 1 if way == 0 else -1),
            )

    def begin(self):
        for way in range(2):
            ref = self.ref(0, 0, None)
            self.copies.start(
                ref, ref, self.send1.at[way, 0], self.recv1.at[way, 0], self.device(1 if way == 0 else -1, 0)
            )
        self.across_send(0)

    def near(self, way):
        towards = 1 if way == 0 else -1
        self.copies.arrived(
            self.ref(-towards, 0, None), self.send1.at[way, 0], self.recv1.at[way, 0], self.device(towards, 0)
        )
        ref = self.ref(-towards, 0, way)
        self.copies.start(
            ref, ref, self.send1.at[way, 1], self.recv1.at[way, 1], self.device(towards, 0)
        )
        self.across_send(1 + way)

    def far(self, way):
        towards = 1 if way == 0 else -1
        self.copies.arrived(
            self.ref(2, 0, way), self.send1.at[way, 1], self.recv1.at[way, 1], self.device(towards, 0)
        )
        self.across_send(3 + way)

    def across_near(self, item):
        for way in range(2):
            towards = 1 if way == 0 else -1
            self.copies.arrived(
                self.ref(self.shift(item), -towards, self.part(item)),
                self.send2.at[item, way, 0],
                self.recv2.at[item, way, 0],
                self.device(0, towards),
            )
            if item < 3 or item - 3 == way:
                ref = self.ref(self.shift(item), -towards, way)
                self.copies.start(
                    ref, ref, self.send2.at[item, way, 1], self.recv2.at[item, way, 1], self.device(0, towards)
                )

    def across_far(self, item):
        for way in range(2):
            if item < 3 or item - 3 == way:
                self.copies.arrived(
                    self.ref(self.shift(item), 2, way),
                    self.send2.at[item, way, 1],
                    self.recv2.at[item, way, 1],
                    self.device(0, 1 if way == 0 else -1),
                )


def gather_kernel(
    table, panel, inv_factor, rhs,
    rows, cols, sides,
    slab, solved, picked, local_sem,
    ring1, ring1_in, mate1, mate1_in,
    ring2, ring2_in, mate2, mate2_in,
    ring3, ring3_in, mate3, mate3_in,
    swap, swap_in, plane1, plane1_in, plane2, plane2_in,
):
    row = lax.axis_index("row")
    col = lax.axis_index("col")
    x, y = row // NY, lax.rem(row, NY)
    z, k = col // 2, lax.rem(col, 2)
    place = (row, z, k)

    loads = []
    for q in range(2):
        for b in range(2):
            load = pltpu.make_async_copy(
                panel.at[q, b, pl.ds(pl.multiple_of(row * SLAB, SLAB), SLAB)], slab.at[q, b], local_sem.at[q, b]
            )
            load.start()
            loads.append(load)

    barrier = pltpu.get_barrier_semaphore()
    partners = [(row, lax.rem(z + 1, NZ) * 2 + k), (row, lax.rem(z + NZ - 1, NZ) * 2 + k), (row, z * 2 + 1 - k)]
    partners += [(lax.rem(row + d, NROW), col) for d in range(1, NROW)]
    for partner in partners:
        pl.semaphore_signal(barrier, inc=1, device_id=partner, device_id_type=MESH)

    solved[ZERO_BLOCK] = jnp.zeros((SLAB, PW), jnp.bfloat16)
    sides[col] = rhs[...]
    for load in loads:
        load.wait()
    for q in range(2):
        block = slab[q].astype(jnp.float32).reshape(2 * SLAB, PW).astype(jnp.bfloat16)
        value = lax.dot_general(
            block, inv_factor[q], (((1,), (1,)), ((), ())), preferred_element_type=jnp.float32
        )
        for b in range(2):
            solved[col * 4 + q * 2 + b] = value[b * SLAB:(b + 1) * SLAB].astype(jnp.bfloat16)

    pl.semaphore_wait(barrier, len(partners))

    copies = Copies()
    slabs = ZRing(
        copies,
        lambda origin: solved.at[pl.ds(origin * 4, 4)],
        lambda origin, way: solved.at[pl.ds(origin * 4 + way * 2, 2)],
        place, ring1, ring1_in, mate1, mate1_in,
    )
    side_ring = ZRing(
        copies,
        lambda origin: sides.at[origin],
        lambda origin, way: sides.at[origin, way],
        place, ring2, ring2_in, mate2, mate2_in,
    )
    row_rings = [
        ZRing(
            copies,
            lambda origin, n=n: rows.at[origin, pl.ds(n * 8, 8)],
            lambda origin, way, n=n: rows.at[origin, pl.ds(n * 8 + way * 4, 4)],
            place, ring3.at[n], ring3_in.at[n], mate3.at[n], mate3_in.at[n],
        )
        for n in range(2)
    ]
    planes = [
        PlaneGather(
            copies, cols, half, (x, y, col), plane1.at[half], plane1_in.at[half], plane2.at[half], plane2_in.at[half]
        )
        for half in range(2)
    ]

    slabs.begin()
    side_ring.begin()
    slabs.step(1)
    slabs.step(2)
    side_ring.step(1)
    slabs.step(3)
    slabs.step(4)
    slabs.end()

    for d in range(1, NROW):
        there = lax.rem(row + d, NROW)
        picked[d] = solved[table[SLOTS + there]]
        copies.start(picked.at[d], rows.at[col, row], swap.at[d], swap_in.at[d], (there, col))
    rows[col, row] = solved[table[SLOTS + row]]
    for slot in range(SLOTS):
        cols[row, slot] = solved[table[slot]]
    for plane in planes:
        plane.begin()
    side_ring.step(2)
    for d in range(1, NROW):
        origin = lax.rem(row + NROW - d, NROW)
        copies.arrived(rows.at[col, origin], swap.at[d], swap_in.at[d], (origin, col))
    for ring in row_rings:
        ring.begin()
    side_ring.step(3)
    for plane in planes:
        plane.near(0)
        plane.near(1)
    for plane in planes:
        plane.across_near(0)
    for ring in row_rings:
        ring.step(1)
    for plane in planes:
        plane.far(0)
        plane.far(1)
    for plane in planes:
        plane.across_near(1)
    for ring in row_rings:
        ring.step(2)
    for plane in planes:
        plane.across_near(2)
    for ring in row_rings:
        ring.step(3)
    for plane in planes:
        plane.across_near(3)
        plane.across_near(4)
    side_ring.step(4)
    for ring in row_rings:
        ring.step(4)
    for item in range(5):
        for plane in planes:
            plane.across_far(item)
    side_ring.end()
    for ring in row_rings:
        ring.end()
    copies.finish()


def gather(table, panel, inv_factor, rhs):
    dma = pltpu.SemaphoreType.DMA
    vmem = pl.BlockSpec(memory_space=pltpu.VMEM)
    return pl.pallas_call(
        gather_kernel,
        out_shape=(
            jax.ShapeDtypeStruct((SLOTS, NROW, SLAB, PW), jnp.bfloat16),
            jax.ShapeDtypeStruct((NROW, SLOTS, SLAB, PW), jnp.bfloat16),
            jax.ShapeDtypeStruct((NCOL,) + rhs.shape, jnp.bfloat16),
        ),
        in_specs=[
            pl.BlockSpec(memory_space=pltpu.SMEM),
            pl.BlockSpec(memory_space=pl.ANY),
            vmem,
            vmem,
        ],
        out_specs=(vmem, vmem, vmem),
        scratch_shapes=[
            pltpu.VMEM((2, 2, SLAB, PW), jnp.bfloat16),
            pltpu.VMEM((ZERO_BLOCK + 1, SLAB, PW), jnp.bfloat16),
            pltpu.VMEM((NROW, SLAB, PW), jnp.bfloat16),
            dma((2, 2)),
            dma((2, 4)), dma((2, 4)), dma((9,)), dma((9,)),
            dma((2, 4)), dma((2, 4)), dma((9,)), dma((9,)),
            dma((2, 2, 4)), dma((2, 2, 4)), dma((2, 9)), dma((2, 9)),
            dma((16,)), dma((16,)),
            dma((2, 2, 2)), dma((2, 2, 2)), dma((2, 5, 2, 2)), dma((2, 5, 2, 2)),
        ],
        compiler_params=pltpu.CompilerParams(
            collective_id=0, has_side_effects=True, vmem_limit_bytes=16 << 20
        ),
        name="gather_blocks",
    )(table, panel, inv_factor, rhs)


def update_kernel(rows, cols, inv_factor, rhs, target, right_sides, out_target, out_sides, partial, factors):
    step = pl.program_id(0)

    @pl.when(step == 0)
    def _():
        for q in range(2):
            value = jnp.dot(
                inv_factor[q], rhs[:, q].reshape(PW, rhs.shape[-1]), preferred_element_type=jnp.float32
            )
            partial[q] = value.astype(jnp.bfloat16)
            for s in range(8):
                factors[q, pl.ds(s * 128, 128), :] = cols[:, q * 8 + s].reshape(128, PW)

    tiles = target.shape[0]
    left = [rows[q].reshape(tiles * 128, PW) for q in range(2)]
    for pair in range(4):
        product = 0.0
        for q in range(2):
            product += lax.dot_general(
                left[q],
                factors[q, pl.ds(pair * 256, 256), :],
                (((1,), (1,)), ((), ())),
                preferred_element_type=jnp.float32,
            )
        for n in range(2):
            s = pair * 2 + n
            for t in range(tiles):
                at = (t, pl.ds(s, 128, 8), slice(None))
                out_target[at] = target[at] - product[t * 128:(t + 1) * 128, n * 128:(n + 1) * 128]
    for n in range(right_sides.shape[0]):
        start = pl.multiple_of((step * right_sides.shape[0] + n) * 128, 128)
        product = 0.0
        for q in range(2):
            product += jnp.dot(
                factors[q, pl.ds(start, 128), :], partial[q], preferred_element_type=jnp.float32
            )
        out_sides[n] = right_sides[n] - product


def update(rows, cols, inv_factor, rhs, target, right_sides):
    steps = 4
    each = 8 // steps
    whole = lambda shape: pl.BlockSpec(shape, lambda i: (0,) * len(shape))
    return pl.pallas_call(
        update_kernel,
        grid=(steps,),
        out_shape=(
            jax.ShapeDtypeStruct(target.shape, jnp.float32),
            jax.ShapeDtypeStruct(right_sides.shape, jnp.float32),
        ),
        in_specs=[
            pl.BlockSpec((2, each, 128, PW), lambda i: (0, i, 0, 0)),
            whole(cols.shape),
            whole(inv_factor.shape),
            whole(rhs.shape),
            pl.BlockSpec((each,) + target.shape[1:], lambda i: (i, 0, 0)),
            pl.BlockSpec((each,) + right_sides.shape[1:], lambda i: (i, 0, 0)),
        ],
        out_specs=(
            pl.BlockSpec((each,) + target.shape[1:], lambda i: (i, 0, 0)),
            pl.BlockSpec((each,) + right_sides.shape[1:], lambda i: (i, 0, 0)),
        ),
        scratch_shapes=[
            pltpu.VMEM((2, PW, rhs.shape[-1]), jnp.bfloat16),
            pltpu.VMEM((2, 1024, PW), jnp.bfloat16),
        ],
        compiler_params=pltpu.CompilerParams(
            dimension_semantics=("arbitrary",), vmem_limit_bytes=24 << 20
        ),
        name="update_blocks",
    )(rows, cols, inv_factor, rhs, target, right_sides)


def block_table(panel_rows):
    col = lax.axis_index("col")
    entry = jnp.arange(2 * SLOTS, dtype=jnp.int32)
    first = entry < SLOTS
    slot = jnp.where(first, entry, col)
    position = (slot % 8) * 16 + jnp.where(first, col, entry - SLOTS)
    panel = slot // 8
    positions = jnp.where((panel == 0)[:, None], panel_rows[0][None], panel_rows[1][None])
    block = jnp.arange(panel_rows.shape[1], dtype=jnp.int32)
    place = (block // 2) * 4 + block % 2
    found = positions == position[:, None]
    return ZERO_BLOCK + jnp.sum(
        jnp.where(found, place[None] + panel[:, None] * 2 - ZERO_BLOCK, 0), axis=1, dtype=jnp.int32
    )


def shards(target, panel_a, inv_factor, panel_rhs, panel_rows, right_sides):
    table = block_table(panel_rows)
    rows, cols, rhs = gather(table, panel_a, inv_factor, panel_rhs)
    new_target, new_sides = update(
        rows.reshape(2, 8, 128, PW),
        cols,
        inv_factor,
        rhs,
        target.reshape(8, 1024, 128),
        right_sides.reshape(8, 128, 256),
    )
    return new_target.reshape(target.shape), new_sides.reshape(right_sides.shape)


def solution(mesh):
    placed = (
        P(None, "row", None, None, "col", None),
        P(None, "col", None, None),
        P(),
        P(None, "col", None),
        P(),
        P(None, "col", None, None),
    )
    return jax.shard_map(
        shards,
        mesh=mesh,
        in_specs=placed,
        out_specs=(P(None, "row", None, None, "col", None), P(None, "col", None, None)),
        check_vma=False,
    )
```

time: 168 us -> 64.2 us (0.38)
  blocking collectives: 118 us -> 0 us
  Pallas kernels: 0 us -> 54.5 us
  matrix products: 25.8 us -> 0 us
  between operations: 14.2 us -> 0.68 us
    psum x1 -> x0, blocking collectives: 77.4 us -> none  [shards(): partial_value = lax.psum(local_term, 'col').astype(jnp.bfloat16)]
    pallas_call x0 -> x2, Pallas kernels: none -> 54.5 us  [the longest x1 48.7 us: gather(): pl.pallas_call(gather_kernel, out_shape=(jax.ShapeDtypeStruct((SLOTS, NRO...]
    all_gather x2 -> x0, blocking collectives: 40.8 us -> none  [shards(): column_tiles = lax.all_gather(solved_piece, 'row', axis=1, tiled=True)]
    dot_general x12 -> x0, matrix products: 25.8 us -> none  [the longest x2 9.25 us: shards(): jnp.einsum('ka,axp->kxp', pick_cols, all_tiles, preferred_element_type=jn...]
    slice x2 -> x0, local copies, waits for them, and re-layouts: 2.34 us -> none  [the longest x1 1.27 us: shards(): factor = inv_factor[which_panel]]
    unnamed x13 -> x12, local copies, waits for them, and re-layouts: 6.87 us -> 7.65 us
  transfers between devices with their start and end apart: 2 -> 0, of which waited for: 0 -> 0; matrix products, arithmetic and copies ran while one was open for 6% -> 0% of each run, Pallas kernels for 0% -> 0%
where the time goes in v1:
time: 64.2 us; the launch traced here: 63.8 us
  Pallas kernels  54.5 us (85%)
  local copies, waits for them, and re-layouts  8.41 us (13%)
  between operations  0.68 us (1%)
    pallas_call x1, Pallas kernels, gather(): pl.pallas_call(gather_kernel, out_shape=(jax.ShapeDtypeStruct((SLOTS, NRO...  48.7 us
    unnamed x12, local copies, waits for them, and re-layouts  7.65 us
    pallas_call x1, Pallas kernels, update(): pl.pallas_call(update_kernel, grid=(steps,), out_shape=(jax.ShapeDtypeStr...  5.84 us

profile of v1, /device:TPU:1, one launch (start us, length us, event | category | flops | bytes accessed | tf_op | source)
XLA Modules:
  0.0 63.8 jit_solution(17160780263945162530)
XLA Ops:
  0.7 0.8 %slice_bitcast_fusion.1 = (s32[32]{0:T(128)S(1)}, s32[32]{0:T(128)S(1)}) fusion(s32[2,32]{1,0:T(2,128)} %param.10), kind=kLoop, calls=%fused_computation.19 | loop fusion | bytes 512 | tf_op jit(solution)/shard_map/jit(_where)/broadcast_in_dim | solution.py:437
  1.4 0.2 select_reduce_fusion
  1.6 0.0 copy-start.1
  1.6 1.2 %copy-done.1 = bf16[2,512,512]{2,1,0:T(8,128)(2,1)S(1)} copy-done((bf16[2,512,512]{2,1,0:T(8,128)(2,1)S(1)}, bf16[2,512,512]{2,1,0:T(8,128)(2,1)}, u32[]{:S(2)}) %copy-start.1) | copy-done | bytes 1048600
  2.9 0.0 copy-start.4
  2.9 1.0 %copy-done.4 = bf16[2,2,128,512]{3,2,1,0:T(8,128)(2,1)S(1)} copy-done((bf16[2,2,128,512]{3,2,1,0:T(8,128)(2,1)S(1)}, bf16[2,2,128,512]{3,2,1,0:T(8,128)(2,1)}, u32[]{:S(2)}) %copy-start.4) | copy-done | bytes 524312
  3.9 0.0 copy-start.5
  3.9 0.8 %copy-done.5 = bf16[2,32,256]{2,1,0:T(8,128)(2,1)S(1)} copy-done((bf16[2,32,256]{2,1,0:T(8,128)(2,1)S(1)}, bf16[2,32,256]{2,1,0:T(8,128)(2,1)}, u32[]{:S(2)}) %copy-start.5) | copy-done | bytes 32792
  4.7 48.7 %gather_blocks.1 = (bf16[16,16,8,512]{3,2,1,0:T(8,128)(2,1)S(1)}, bf16[16,16,8,512]{3,2,1,0:T(8,128)(2,1)S(1)}, bf16[16,2,32,256]{3,2,1,0:T(8,128)(2,1)S(1)}) custom-call(s32[32]{0:T(128)S(1)} %broadcast_add_fusion.table, bf16[2,2,128,512]{3,2,1,0:T(8,128)(2,1)S(1)} %copy-done.4, bf16[2,512,512]{2,1,0:T(8,128)(2,1)S(1)} %copy-done.1, ...), custom_call_target="tpu_custom_call" | custom-call | tf_op jit(solution)/shard_map/gather_blocks/pallas_call | solution.py:325
  53.4 0.0 copy-start
  53.4 2.2 %copy-done = f32[8,1,128,8,1,128]{5,4,3,2,1,0:T(1,128)S(1)} copy-done((f32[8,1,128,8,1,128]{5,4,3,2,1,0:T(1,128)S(1)}, f32[8,1,128,8,1,128]{5,4,3,2,1,0:T(1,128)}, u32[]{:S(2)}) %copy-start) | copy-done | bytes 4194328
  55.6 0.0 copy-start.2
  55.6 1.2 %copy-done.2 = bf16[2,512,512]{2,1,0:T(8,128)(2,1)S(1)} copy-done((bf16[2,512,512]{2,1,0:T(8,128)(2,1)S(1)}, bf16[2,512,512]{2,1,0:T(8,128)(2,1)}, u32[]{:S(2)}) %copy-start.2) | copy-done | bytes 1048600
  56.8 0.0 copy-start.3
  56.8 1.2 %copy-done.3 = f32[8,1,128,256]{3,2,1,0:T(8,128)S(1)} copy-done((f32[8,1,128,256]{3,2,1,0:T(8,128)S(1)}, f32[8,1,128,256]{3,2,1,0:T(8,128)}, u32[]{:S(2)}) %copy-start.3) | copy-done | bytes 1048600
  58.0 5.8 %update_blocks.1 = (f32[8,1024,128]{2,1,0:T(8,128)}, f32[8,128,256]{2,1,0:T(8,128)}) custom-call(bf16[2,8,128,512]{3,2,1,0:T(8,128)(2,1)S(1)} %bitcast.14, bf16[16,16,8,512]{3,2,1,0:T(8,128)(2,1)S(1)} %get-tuple-element.8.cols, bf16[2,512,512]{2,1,0:T(8,128)(2,1)S(1)} %copy-done.2, bf16[16,2,32,256]{3,2,1,0:T(8,128)(2,1)S(1)} %get-tuple-element.9.rhs, ...), custom_call_target="tpu_custom_call" | custom-call | tf_op jit(solution)/shard_map/update_blocks/pallas_call | solution.py:400
  (4 shorter events, 0.0 us)
Async XLA Ops:
  1.6 1.2 %copy-start.1 = (bf16[2,512,512]{2,1,0:T(8,128)(2,1)S(1)}, bf16[2,512,512]{2,1,0:T(8,128)(2,1)}, u32[]{:S(2)}) copy-start(bf16[2,512,512]{2,1,0:T(8,128)(2,1)} %inv_factor.3) | copy-start | bytes 3145732
  2.9 1.0 %copy-start.4 = (bf16[2,2,128,512]{3,2,1,0:T(8,128)(2,1)S(1)}, bf16[2,2,128,512]{3,2,1,0:T(8,128)(2,1)}, u32[]{:S(2)}) copy-start(bf16[2,2,128,512]{3,2,1,0:T(8,128)(2,1)} %panel.1) | copy-start | bytes 1572868
  3.9 0.8 %copy-start.5 = (bf16[2,32,256]{2,1,0:T(8,128)(2,1)S(1)}, bf16[2,32,256]{2,1,0:T(8,128)(2,1)}, u32[]{:S(2)}) copy-start(bf16[2,32,256]{2,1,0:T(8,128)(2,1)} %rhs.1) | copy-start | bytes 98308
  53.4 2.2 %copy-start = (f32[8,1,128,8,1,128]{5,4,3,2,1,0:T(1,128)S(1)}, f32[8,1,128,8,1,128]{5,4,3,2,1,0:T(1,128)}, u32[]{:S(2)}) copy-start(f32[8,1,128,8,1,128]{5,4,3,2,1,0:T(1,128)} %param.6) | copy-start | bytes 12582916
  55.6 1.2 %copy-start.2 = (bf16[2,512,512]{2,1,0:T(8,128)(2,1)S(1)}, bf16[2,512,512]{2,1,0:T(8,128)(2,1)}, u32[]{:S(2)}) copy-start(bf16[2,512,512]{2,1,0:T(8,128)(2,1)} %inv_factor.3) | copy-start | bytes 3145732
  56.8 1.2 %copy-start.3 = (f32[8,1,128,256]{3,2,1,0:T(8,128)S(1)}, f32[8,1,128,256]{3,2,1,0:T(8,128)}, u32[]{:S(2)}) copy-start(f32[8,1,128,256]{3,2,1,0:T(8,128)} %param.11) | copy-start | bytes 3145732

commit v2 on v0

v2 whole, which is shorter than its diff:
```python
import functools

import jax
import jax.numpy as jnp
from jax import lax
from jax.experimental import pallas as pl
from jax.experimental.pallas import tpu as pltpu
from jax.sharding import PartitionSpec as P

MESH = pl.DeviceIdType.MESH
NX, NY, NZ = 4, 4, 8
NROW, NCOL = 16, 16
SLAB = 8
PW = 512
NRHS = 256
TILE = 128
ZERO_BLOCK = 64
NEAREST = (1, 7, 2, 6, 3, 5, 4)


def remote(src, dst, send_sem, recv_sem, device):
    return pltpu.make_async_remote_copy(
        src_ref=src, dst_ref=dst, send_sem=send_sem, recv_sem=recv_sem, device_id=device, device_id_type=MESH
    )


class Copies:
    def __init__(self):
        self.sent = []

    def start(self, ref, send_sem, recv_sem, device):
        copy = remote(ref, ref, send_sem, recv_sem, device)
        copy.start()
        self.sent.append(copy)

    def arrived(self, ref, send_sem, recv_sem, device):
        remote(ref, ref, send_sem, recv_sem, device).wait_recv()

    def finish(self):
        for copy in self.sent:
            copy.wait_send()


class ZGather:
    def __init__(self, copies, piece, place, send, recv, mate_send, mate_recv):
        self.copies, self.piece = copies, piece
        self.row, self.z, self.k = place
        self.send, self.recv = send, recv
        self.mate_send, self.mate_recv = mate_send, mate_recv
        self.mate = (self.row, self.z * 2 + 1 - self.k)

    def chip(self, distance):
        return lax.rem(self.z + distance + NZ, NZ)

    def begin(self):
        own = self.piece(self.z * 2 + self.k)
        for d in NEAREST:
            self.copies.start(own, self.send.at[d], self.recv.at[d], (self.row, self.chip(d) * 2 + self.k))
        self.copies.start(own, self.mate_send.at[0], self.mate_recv.at[0], self.mate)

    def collect(self):
        for d in NEAREST:
            ref = self.piece(self.chip(-d) * 2 + self.k)
            self.copies.arrived(ref, self.send.at[d], self.recv.at[d], (self.row, self.chip(d) * 2 + self.k))
            self.copies.start(ref, self.mate_send.at[d], self.mate_recv.at[d], self.mate)

    def end(self):
        for d in (0,) + NEAREST:
            ref = self.piece(self.chip(-d) * 2 + 1 - self.k)
            self.copies.arrived(ref, self.mate_send.at[d], self.mate_recv.at[d], self.mate)


class PlaneGather:
    def __init__(self, copies, cols, half, place, send1, recv1, send2, recv2):
        self.copies, self.cols, self.half = copies, cols, half
        self.x, self.y, self.col = place
        self.send1, self.recv1, self.send2, self.recv2 = send1, recv1, send2, recv2
        count = cols.shape[1] // 2
        self.count, self.lead = count, (count + 1) // 2

    def row(self, along, across):
        dx, dy = (along, across) if self.half == 0 else (across, along)
        return lax.rem(self.x + dx + NX, NX) * NY + lax.rem(self.y + dy + NY, NY)

    def device(self, along, across):
        return (self.row(along, across), self.col)

    def ref(self, along, across, part):
        start = self.half * self.count + (self.lead if part == 1 else 0)
        size = {None: self.count, 0: self.lead, 1: self.count - self.lead}[part]
        return self.cols.at[self.row(along, across), pl.ds(start, size)]

    def shift(self, item):
        return (0, -1, 1, 2, 2)[item]

    def part(self, item):
        return (None, None, None, 0, 1)[item]

    def across_send(self, item):
        for way in range(2):
            self.copies.start(
                self.ref(self.shift(item), 0, self.part(item)),
                self.send2.at[item, way, 0],
                self.recv2.at[item, way, 0],
                self.device(0, 1 if way == 0 else -1),
            )

    def begin(self):
        for way in range(2):
            self.copies.start(
                self.ref(0, 0, None), self.send1.at[way, 0], self.recv1.at[way, 0], self.device(1 if way == 0 else -1, 0)
            )
        self.across_send(0)

    def near(self, way):
        towards = 1 if way == 0 else -1
        self.copies.arrived(
            self.ref(-towards, 0, None), self.send1.at[way, 0], self.recv1.at[way, 0], self.device(towards, 0)
        )
        self.copies.start(
            self.ref(-towards, 0, way), self.send1.at[way, 1], self.recv1.at[way, 1], self.device(towards, 0)
        )
        self.across_send(1 + way)

    def far(self, way):
        towards = 1 if way == 0 else -1
        self.copies.arrived(
            self.ref(2, 0, way), self.send1.at[way, 1], self.recv1.at[way, 1], self.device(towards, 0)
        )
        self.across_send(3 + way)

    def across_near(self, item):
        for way in range(2):
            towards = 1 if way == 0 else -1
            self.copies.arrived(
                self.ref(self.shift(item), -towards, self.part(item)),
                self.send2.at[item, way, 0],
                self.recv2.at[item, way, 0],
                self.device(0, towards),
            )
            if item < 3 or item - 3 == way:
                self.copies.start(
                    self.ref(self.shift(item), -towards, way),
                    self.send2.at[item, way, 1],
                    self.recv2.at[item, way, 1],
                    self.device(0, towards),
                )

    def across_far(self, item):
        for way in range(2):
            if item < 3 or item - 3 == way:
                self.copies.arrived(
                    self.ref(self.shift(item), 2, way),
                    self.send2.at[item, way, 1],
                    self.recv2.at[item, way, 1],
                    self.device(0, 1 if way == 0 else -1),
                )


def class_tables(panel_rows):
    count = panel_rows.shape[1]
    shape = (count, count)
    down = lax.broadcasted_iota(jnp.int32, shape, 0)
    across = lax.broadcasted_iota(jnp.int32, shape, 1)
    lane = lax.broadcasted_iota(jnp.int32, (count, 256), 1)
    block = lax.broadcasted_iota(jnp.int32, (count, 256), 0)
    wide = [jnp.broadcast_to(panel_rows[q:q + 1], shape) for q in range(2)]
    tall = [jnp.sum(jnp.where(down == across, w, 0), axis=1, keepdims=True) for w in wide]
    place, info, total = ZERO_BLOCK, 0, 0
    for q in range(2):
        same = (tall[q] & 15) == (wide[q] & 15)
        rank = jnp.sum(jnp.where(same & (across < down), 1, 0), axis=1, keepdims=True)
        if q == 1:
            rank += jnp.sum(jnp.where((tall[1] & 15) == (wide[0] & 15), 1, 0), axis=1, keepdims=True)
        hit = jnp.broadcast_to((tall[q] & 15) * 16 + rank, lane.shape) == lane
        where_from = (block >> 1) * 4 + (block & 1) + q * 2
        place += jnp.sum(jnp.where(hit, where_from - ZERO_BLOCK, 0), axis=0, keepdims=True)
        spot = jnp.broadcast_to((tall[q] >> 4) + q * 8, lane.shape)
        info += jnp.sum(jnp.where(hit, spot, 0), axis=0, keepdims=True)
        member = jnp.broadcast_to(tall[q] & 15, lane.shape) == (lane >> 4)
        total += jnp.sum(jnp.where(member, 1, 0), axis=0, keepdims=True)
    return place, info, total


def gather_kernel(
    slots,
    positions_hbm, panel, inv_hbm, rhs, target, right_sides,
    rows, cols, partial, meta, target_copy, sides_copy,
    positions, slab, inv_factor, solved, picked, sides, table, local_sem,
    z1, z1_in, mate1, mate1_in, z2, z2_in, mate2, mate2_in,
    swap, swap_in, hand, hand_in, plane1, plane1_in, plane2, plane2_in,
):
    row = lax.axis_index("row")
    col = lax.axis_index("col")
    x, y = row // NY, lax.rem(row, NY)
    z, k = col // 2, lax.rem(col, 2)
    place = (row, z, k)
    mate = (row, z * 2 + 1 - k)

    def load(src, dst, n):
        copy = pltpu.make_async_copy(src, dst, local_sem.at[n])
        copy.start()
        return copy

    own_rows = pl.ds(pl.multiple_of(row * SLAB, SLAB), SLAB)
    first = [load(panel.at[q, b, own_rows], slab.at[q, b], 2 * q + b) for q in range(2) for b in range(2)]
    first += [load(inv_hbm, inv_factor, 4)]
    second = [load(rhs, sides.at[col], 5), load(positions_hbm, positions, 9)]

    barrier = pltpu.get_barrier_semaphore()
    partners = [(row, lax.rem(z + d, NZ) * 2 + k) for d in NEAREST] + [mate]
    partners += [(lax.rem(row + d, NROW), col) for d in range(1, NROW)]
    for partner in partners:
        pl.semaphore_signal(barrier, inc=1, device_id=partner, device_id_type=MESH)

    solved[ZERO_BLOCK] = jnp.zeros((SLAB, PW), jnp.bfloat16)
    for copy in first:
        copy.wait()
    for q in range(2):
        block = slab[q].astype(jnp.float32).reshape(2 * SLAB, PW).astype(jnp.bfloat16)
        value = lax.dot_general(
            block, inv_factor[q], (((1,), (1,)), ((), ())), preferred_element_type=jnp.float32
        )
        for b in range(2):
            solved[col * 4 + q * 2 + b] = value[b * SLAB:(b + 1) * SLAB].astype(jnp.bfloat16)
    for copy in second:
        copy.wait()

    pl.semaphore_wait(barrier, len(partners))

    copies = Copies()
    slabs = ZGather(
        copies, lambda origin: solved.at[pl.ds(origin * 4, 4)], place, z1, z1_in, mate1, mate1_in
    )
    side_parts = ZGather(copies, lambda origin: sides.at[origin], place, z2, z2_in, mate2, mate2_in)
    planes = [
        PlaneGather(
            copies, cols, half, (x, y, col), plane1.at[half], plane1_in.at[half], plane2.at[half], plane2_in.at[half]
        )
        for half in range(2)
    ]

    slabs.begin()
    side_parts.begin()
    late = [load(target, target_copy, 6), load(right_sides, sides_copy, 7)]
    for n, values in enumerate(class_tables(positions[...])):
        meta[n:n + 1, :] = values
    to_scalars = load(meta, table, 8)
    to_scalars.wait()
    slabs.collect()
    slabs.end()

    for slot in range(slots):
        cols[row, slot] = solved[table[0, col * 16 + slot]]
    for plane in planes:
        plane.begin()

    share = slots // 2
    own_share = pl.ds(k * share, share)

    def send_picked(d, carry):
        there = lax.rem(row + d, NROW)
        for j in range(share):
            picked[d, j] = solved[table[0, there * 16 + k * share + j]]
        remote(picked.at[d], rows.at[row, own_share], swap.at[d], swap_in.at[d], (there, col)).start()
        return carry

    lax.fori_loop(1, NROW, send_picked, 0)
    for j in range(share):
        rows[row, k * share + j] = solved[table[0, row * 16 + k * share + j]]

    def hand_over(origin, d):
        ref = rows.at[origin, own_share]
        remote(ref, ref, hand.at[d], hand_in.at[d], mate).start()

    def receive_picked(d, carry):
        origin = lax.rem(row + NROW - d, NROW)
        ref = rows.at[origin, own_share]
        remote(picked.at[d], ref, swap.at[d], swap_in.at[d], (lax.rem(row + d, NROW), col)).wait()
        hand_over(origin, d)
        return carry

    hand_over(row, 0)
    for plane in planes:
        plane.near(0)
        plane.near(1)
    side_parts.collect()
    for plane in planes:
        plane.across_near(0)
    for plane in planes:
        plane.far(0)
        plane.far(1)
    for plane in planes:
        plane.across_near(1)
        plane.across_near(2)
    lax.fori_loop(1, NROW, receive_picked, 0)
    for plane in planes:
        plane.across_near(3)
        plane.across_near(4)
    side_parts.end()
    for q in range(2):
        value = jnp.dot(
            inv_factor[q], sides[:, q].reshape(PW, NRHS), preferred_element_type=jnp.float32
        )
        partial[q] = value.astype(jnp.bfloat16)

    def take_over(d, carry):
        origin = lax.rem(row + NROW - d, NROW)
        ref = rows.at[origin, pl.ds((1 - k) * share, share)]
        remote(ref, ref, hand.at[d], hand_in.at[d], mate).wait()
        return carry

    lax.fori_loop(0, NROW, take_over, 0)
    for item in range(5):
        for plane in planes:
            plane.across_far(item)
    for copy in late:
        copy.wait()
    copies.finish()


def gather(slots, panel_rows, panel, inv_factor, rhs, target, right_sides):
    dma = pltpu.SemaphoreType.DMA
    vmem = pl.BlockSpec(memory_space=pltpu.VMEM)
    hbm = pl.BlockSpec(memory_space=pltpu.MemorySpace.HBM)
    return pl.pallas_call(
        functools.partial(gather_kernel, slots),
        out_shape=(
            jax.ShapeDtypeStruct((NROW, slots, SLAB, PW), jnp.bfloat16),
            jax.ShapeDtypeStruct((NROW, slots, SLAB, PW), jnp.bfloat16),
            jax.ShapeDtypeStruct((2, PW, NRHS), jnp.bfloat16),
            jax.ShapeDtypeStruct((8, 256), jnp.int32),
            jax.ShapeDtypeStruct(target.shape, jnp.float32),
            jax.ShapeDtypeStruct(right_sides.shape, jnp.float32),
        ),
        in_specs=[hbm] * 6,
        out_specs=(vmem,) * 6,
        scratch_shapes=[
            pltpu.VMEM(panel_rows.shape, jnp.int32),
            pltpu.VMEM((2, 2, SLAB, PW), jnp.bfloat16),
            pltpu.VMEM((2, PW, PW), jnp.bfloat16),
            pltpu.VMEM((ZERO_BLOCK + 1, SLAB, PW), jnp.bfloat16),
            pltpu.VMEM((NROW, slots // 2, SLAB, PW), jnp.bfloat16),
            pltpu.VMEM((NCOL,) + rhs.shape, jnp.bfloat16),
            pltpu.SMEM((8, 256), jnp.int32),
            dma((10,)),
            dma((8,)), dma((8,)), dma((8,)), dma((8,)),
            dma((8,)), dma((8,)), dma((8,)), dma((8,)),
            dma((16,)), dma((16,)), dma((16,)), dma((16,)),
            dma((2, 2, 2)), dma((2, 2, 2)), dma((2, 5, 2, 2)), dma((2, 5, 2, 2)),
        ],
        compiler_params=pltpu.CompilerParams(
            collective_id=0, has_side_effects=True, vmem_limit_bytes=24 << 20
        ),
        name="gather_blocks",
    )(
        *[
            pltpu.with_memory_space_constraint(array, pltpu.MemorySpace.HBM)
            for array in (panel_rows, panel, inv_factor, rhs, target, right_sides)
        ]
    )


def update_kernel(
    slots,
    meta, rows, cols, partial, target, right_sides,
    out_target, out_sides,
    tiles, sides, left, right, tile_sem, side_sem,
):
    row = lax.axis_index("row") * 16
    col = lax.axis_index("col") * 16
    rows_here = meta[2, row]
    cols_here = meta[2, col]
    count = target.shape[0]

    def touched(base, total):
        bits = jnp.int32(0)
        for i in range(slots):
            bits |= jnp.where(i < total, jnp.int32(1) << (meta[1, base + i] & 7), 0)
        return bits

    row_bits = touched(row, rows_here)

    def send_tile(source, t):
        return pltpu.make_async_copy(source.at[t], out_target.at[t], tile_sem.at[t])

    for t in range(count):
        @pl.when(((row_bits >> t) & 1) == 0)
        def _():
            send_tile(target, t).start()

        @pl.when(((row_bits >> t) & 1) == 1)
        def _():
            tiles[t] = target[t]

    for i in range(slots):
        @pl.when(i < ((rows_here + 1) // 2) * 2)
        def _():
            left[i * TILE:(i + 1) * TILE, :] = rows[:, i].reshape(TILE, PW)

        @pl.when(i < ((cols_here + 1) // 2) * 2)
        def _():
            right[i * TILE:(i + 1) * TILE, :] = cols[:, i].reshape(TILE, PW)

    sides[...] = right_sides[...]

    def column_pair(jp, carry):
        factor = right[pl.ds(pl.multiple_of(jp * 256, 256), 256), :]

        def row_pair(ip, carry):
            product = lax.dot_general(
                left[pl.ds(pl.multiple_of(ip * 256, 256), 256), :],
                factor,
                (((1,), (1,)), ((), ())),
                preferred_element_type=jnp.float32,
            )
            for a in range(2):
                for b in range(2):
                    i, j = ip * 2 + a, jp * 2 + b
                    left_at, right_at = meta[1, row + i], meta[1, col + j]
                    real = (i < rows_here) & (j < cols_here) & ((left_at >> 3) == (right_at >> 3))

                    @pl.when(real)
                    def _():
                        at = (left_at & 7, pl.ds(right_at & 7, TILE, 8), slice(None))
                        tiles[at] = tiles[at] - product[a * TILE:(a + 1) * TILE, b * TILE:(b + 1) * TILE]

            return carry

        return lax.fori_loop(0, (rows_here + 1) // 2, row_pair, carry)

    lax.fori_loop(0, (cols_here + 1) // 2, column_pair, 0)

    for t in range(count):
        @pl.when(((row_bits >> t) & 1) == 1)
        def _():
            send_tile(tiles, t).start()

    def side(j, carry):
        at = meta[1, col + j]
        product = jnp.dot(
            right[pl.ds(pl.multiple_of(j * TILE, TILE), TILE), :],
            partial[at >> 3],
            preferred_element_type=jnp.float32,
        )
        sides[at & 7] = sides[at & 7] - product
        return carry

    lax.fori_loop(0, cols_here, side, 0)
    last = pltpu.make_async_copy(sides, out_sides, side_sem)
    last.start()
    for t in range(count):
        send_tile(tiles, t).wait()
    last.wait()


def update(slots, meta, rows, cols, partial, target, right_sides):
    vmem = pl.BlockSpec(memory_space=pltpu.VMEM)
    hbm = pl.BlockSpec(memory_space=pltpu.MemorySpace.HBM)
    return pl.pallas_call(
        functools.partial(update_kernel, slots),
        out_shape=(
            jax.ShapeDtypeStruct(target.shape, jnp.float32),
            jax.ShapeDtypeStruct(right_sides.shape, jnp.float32),
        ),
        in_specs=[pl.BlockSpec(memory_space=pltpu.SMEM)] + [vmem] * 5,
        out_specs=(hbm, hbm),
        scratch_shapes=[
            pltpu.VMEM(target.shape, jnp.float32),
            pltpu.VMEM(right_sides.shape, jnp.float32),
            pltpu.VMEM((slots * TILE, PW), jnp.bfloat16),
            pltpu.VMEM((slots * TILE, PW), jnp.bfloat16),
            pltpu.SemaphoreType.DMA((8,)),
            pltpu.SemaphoreType.DMA,
        ],
        compiler_params=pltpu.CompilerParams(vmem_limit_bytes=30 << 20),
        name="update_blocks",
    )(meta, rows, cols, partial, target, right_sides)


def shards(target, panel_a, inv_factor, panel_rhs, panel_rows, right_sides):
    slots = 16
    rows, cols, partial, meta, near_target, near_sides = gather(
        slots,
        panel_rows,
        panel_a,
        inv_factor,
        panel_rhs,
        target.reshape(8, 1024, 128),
        right_sides.reshape(8, 128, 256),
    )
    new_target, new_sides = update(slots, meta, rows, cols, partial, near_target, near_sides)
    return new_target.reshape(target.shape), new_sides.reshape(right_sides.shape)


def solution(mesh):
    placed = (
        P(None, "row", None, None, "col", None),
        P(None, "col", None, None),
        P(),
        P(None, "col", None),
        P(),
        P(None, "col", None, None),
    )
    return jax.shard_map(
        shards,
        mesh=mesh,
        in_specs=placed,
        out_specs=(P(None, "row", None, None, "col", None), P(None, "col", None, None)),
        check_vma=False,
    )
```

time: 168 us -> 58.8 us (0.35)
  the two profiles are of different devices: /device:TPU:1 before, /device:TPU:35 now
where the time goes in v2:
time: 58.8 us; the launch traced here: 58.7 us
  Pallas kernels  58 us (99%)
  between operations  0.64 us (1%)
    pallas_call x1, Pallas kernels, gather(): pl.pallas_call(functools.partial(gather_kernel, slots), out_shape=(jax.Sh...  51.7 us
    pallas_call x1, Pallas kernels, update(): pl.pallas_call(functools.partial(update_kernel, slots), out_shape=(jax.Sh...  6.27 us

profile of v2, /device:TPU:35, one launch (start us, length us, event | category | flops | bytes accessed | tf_op | source)
XLA Modules:
  0.0 58.7 jit_solution(10718296771025291691)
XLA Ops:
  0.6 51.7 %gather_blocks.1 = (bf16[16,16,8,512]{3,2,1,0:T(8,128)(2,1)S(1)}, bf16[16,16,8,512]{3,2,1,0:T(8,128)(2,1)S(1)}, bf16[2,512,256]{2,1,0:T(8,128)(2,1)S(1)}, s32[8,...) custom-call(s32[2,32]{1,0:T(2,128)} %positions_hbm.1, bf16[2,2,128,512]{3,2,1,0:T(8,128)(2,1)} %panel.1, ...), custom_call_target="tpu_custom_call" | custom-call | tf_op jit(solution)/shard_map/gather_blocks/pallas_call | solution.py:326
  52.4 6.3 %update_blocks.1 = (f32[8,1024,128]{2,1,0:T(8,128)}, f32[8,128,256]{2,1,0:T(8,128)}) custom-call(s32[8,256]{1,0:T(8,128)S(1)} %get-tuple-element.10.meta, bf16[16,16,8,512]{3,2,1,0:T(8,128)(2,1)S(1)} %get-tuple-element.11.rows, bf16[16,16,8,512]{3,2,1,0:T(8,128)(2,1)S(1)} %get-tuple-element.12.cols, bf16[2,512,256]{2,1,0:T(8,128)(2,1)S(1)} %get-tuple-element.13.partial, ...), custom_call_target="tpu_custom_call" | custom-call | tf_op jit(solution)/shard_map/update_blocks/pallas_call | solution.py:460

commit v3 on v2

--- a/solution.py
+++ b/solution.py
@@ -179,7 +179,8 @@
         info += jnp.sum(jnp.where(hit, spot, 0), axis=0, keepdims=True)
         member = jnp.broadcast_to(tall[q] & 15, lane.shape) == (lane >> 4)
         total += jnp.sum(jnp.where(member, 1, 0), axis=0, keepdims=True)
-    return place, info, total
+    most = jnp.broadcast_to(jnp.max(total, axis=1, keepdims=True), total.shape)
+    return place, info, total, most
 
 
 def gather_kernel(
@@ -319,7 +320,7 @@
     copies.finish()
 
 
-def gather(slots, panel_rows, panel, inv_factor, rhs, target, right_sides):
+def gather(slots, number, panel_rows, panel, inv_factor, rhs, target, right_sides):
     dma = pltpu.SemaphoreType.DMA
     vmem = pl.BlockSpec(memory_space=pltpu.VMEM)
     hbm = pl.BlockSpec(memory_space=pltpu.MemorySpace.HBM)
@@ -350,7 +351,7 @@
             dma((2, 2, 2)), dma((2, 2, 2)), dma((2, 5, 2, 2)), dma((2, 5, 2, 2)),
         ],
         compiler_params=pltpu.CompilerParams(
-            collective_id=0, has_side_effects=True, vmem_limit_bytes=24 << 20
+            collective_id=number, has_side_effects=True, vmem_limit_bytes=24 << 20
         ),
         name="gather_blocks",
     )(
@@ -365,7 +366,7 @@
     slots,
     meta, rows, cols, partial, target, right_sides,
     out_target, out_sides,
-    tiles, sides, left, right, tile_sem, side_sem,
+    tiles, sides, left, right, product, tile_sem, side_sem,
 ):
     row = lax.axis_index("row") * 16
     col = lax.axis_index("col") * 16
@@ -404,30 +405,36 @@
 
     sides[...] = right_sides[...]
 
+    half = slots // 2
+
     def column_pair(jp, carry):
         factor = right[pl.ds(pl.multiple_of(jp * 256, 256), 256), :]
-
-        def row_pair(ip, carry):
-            product = lax.dot_general(
-                left[pl.ds(pl.multiple_of(ip * 256, 256), 256), :],
-                factor,
-                (((1,), (1,)), ((), ())),
-                preferred_element_type=jnp.float32,
-            )
-            for a in range(2):
-                for b in range(2):
-                    i, j = ip * 2 + a, jp * 2 + b
-                    left_at, right_at = meta[1, row + i], meta[1, col + j]
-                    real = (i < rows_here) & (j < cols_here) & ((left_at >> 3) == (right_at >> 3))
-
-                    @pl.when(real)
-                    def _():
-                        at = (left_at & 7, pl.ds(right_at & 7, TILE, 8), slice(None))
-                        tiles[at] = tiles[at] - product[a * TILE:(a + 1) * TILE, b * TILE:(b + 1) * TILE]
-
-            return carry
-
-        return lax.fori_loop(0, (rows_here + 1) // 2, row_pair, carry)
+        for part in range(2):
+            @pl.when(part * half < rows_here)
+            def _():
+                product[...] = lax.dot_general(
+                    left[part * half * TILE:(part + 1) * half * TILE, :],
+                    factor,
+                    (((1,), (1,)), ((), ())),
+                    preferred_element_type=jnp.float32,
+                )
+
+                def subtract(i, carry):
+                    left_at = meta[1, row + part * half + i]
+                    for b in range(2):
+                        right_at = meta[1, col + jp * 2 + b]
+
+                        @pl.when((jp * 2 + b < cols_here) & ((left_at >> 3) == (right_at >> 3)))
+                        def _():
+                            at = (left_at & 7, pl.ds(right_at & 7, TILE, 8), slice(None))
+                            block = product[pl.ds(pl.multiple_of(i * TILE, TILE), TILE), b * TILE:(b + 1) * TILE]
+                            tiles[at] = tiles[at] - block
+
+                    return carry
+
+                lax.fori_loop(0, jnp.minimum(rows_here - part * half, half), subtract, 0)
+
+        return carry
 
     lax.fori_loop(0, (cols_here + 1) // 2, column_pair, 0)
 
@@ -470,6 +477,7 @@
             pltpu.VMEM(right_sides.shape, jnp.float32),
             pltpu.VMEM((slots * TILE, PW), jnp.bfloat16),
             pltpu.VMEM((slots * TILE, PW), jnp.bfloat16),
+            pltpu.VMEM((slots // 2 * TILE, 2 * TILE), jnp.float32),
             pltpu.SemaphoreType.DMA((8,)),
             pltpu.SemaphoreType.DMA,
         ],
@@ -479,17 +487,18 @@
 
 
 def shards(target, panel_a, inv_factor, panel_rhs, panel_rows, right_sides):
-    slots = 16
-    rows, cols, partial, meta, near_target, near_sides = gather(
-        slots,
-        panel_rows,
-        panel_a,
-        inv_factor,
-        panel_rhs,
-        target.reshape(8, 1024, 128),
-        right_sides.reshape(8, 128, 256),
-    )
-    new_target, new_sides = update(slots, meta, rows, cols, partial, near_target, near_sides)
+    few, most = 10, 16
+    args = (panel_rows, panel_a, inv_factor, panel_rhs, target.reshape(8, 1024, 128), right_sides.reshape(8, 128, 256))
+    rows, cols, partial, meta, near_target, near_sides = gather(few, 0, *args)
+
+    def usual():
+        return update(few, meta, rows, cols, partial, near_target, near_sides)
+
+    def crowded():
+        rows, cols, partial, meta, near_target, near_sides = gather(most, 1, *args)
+        return update(most, meta, rows, cols, partial, near_target, near_sides)
+
+    new_target, new_sides = lax.cond(meta[3, 0] <= few, usual, crowded)
     return new_target.reshape(target.shape), new_sides.reshape(right_sides.shape)
 
 

time: 58.8 us -> 51.6 us (0.88)
  the two profiles are of different devices: /device:TPU:35 before, /device:TPU:1 now
where the time goes in v3:
time: 51.6 us; the launch traced here: 51.5 us
  Pallas kernels  49.7 us (96%)
  between operations  1.29 us (2%)
    pallas_call x1, Pallas kernels, gather(): pl.pallas_call(functools.partial(gather_kernel, slots), out_shape=(jax.Sh...  43 us
    pallas_call x1, Pallas kernels, update(): pl.pallas_call(functools.partial(update_kernel, slots), out_shape=(jax.Sh...  6.63 us

profile of v3, /device:TPU:1, one launch (start us, length us, event | category | flops | bytes accessed | tf_op | source)
XLA Modules:
  0.0 51.5 jit_solution(9273260613350995020)
XLA Ops:
  0.6 43.0 %gather_blocks.3 = (bf16[16,10,8,512]{3,2,1,0:T(8,128)(2,1)S(1)}, bf16[16,10,8,512]{3,2,1,0:T(8,128)(2,1)S(1)}, bf16[2,512,256]{2,1,0:T(8,128)(2,1)S(1)}, s32[8,...) custom-call(s32[2,32]{1,0:T(2,128)} %positions_hbm.1, bf16[2,2,128,512]{3,2,1,0:T(8,128)(2,1)} %panel.1, ...), custom_call_target="tpu_custom_call" | custom-call | tf_op jit(solution)/shard_map/gather_blocks/pallas_call | solution.py:327
  43.7 0.5 slice.3
  44.8 6.6 %conditional.1 = ((f32[8,1024,128]{2,1,0:T(8,128)}, f32[8,128,256]{2,1,0:T(8,128)})) conditional(s32[]{:T(128)} %bitcast.2, (s32[2,32]{1,0:T(2,128)}, bf16[2,2,128,512]{3,2,1,0:T(8,128)(2,1)}, bf16[2,512,512]{2,1,0:T(8,128)(2,1)}, bf16[2,32,256]{2,1,0:T(8,128)(2,1)}, f32[8,1024,128]{2,1,0:T(8,128)}, /*index=5*/f32[8,128,256]{2,1,0:T(8,128)}) %tuple.29, ...), branch_computations={%region_0.0_spmd, %region_1.0_spmd} | conditional | bytes 8 | solution.py:501
  44.9 6.6 %update_blocks.3 = (f32[8,1024,128]{2,1,0:T(8,128)}, f32[8,128,256]{2,1,0:T(8,128)}) custom-call(s32[8,256]{1,0:T(8,128)S(1)} %get-tuple-element.44.meta, bf16[16,10,8,512]{3,2,1,0:T(8,128)(2,1)S(1)} %get-tuple-element.45.rows, bf16[16,10,8,512]{3,2,1,0:T(8,128)(2,1)S(1)} %get-tuple-element.46.cols, bf16[2,512,256]{2,1,0:T(8,128)(2,1)S(1)} %get-tuple-element.47.partial, ...), custom_call_target="tpu_custom_call" | custom-call | tf_op jit(solution)/shard_map/cond/branch_1_fun/update_blocks/pallas_call | solution.py:467

commit v4 on v3

--- a/solution.py
+++ b/solution.py
@@ -179,8 +179,10 @@
         info += jnp.sum(jnp.where(hit, spot, 0), axis=0, keepdims=True)
         member = jnp.broadcast_to(tall[q] & 15, lane.shape) == (lane >> 4)
         total += jnp.sum(jnp.where(member, 1, 0), axis=0, keepdims=True)
+        if q == 0:
+            lead = total
     most = jnp.broadcast_to(jnp.max(total, axis=1, keepdims=True), total.shape)
-    return place, info, total, most
+    return place, info, total, most, lead
 
 
 def gather_kernel(
@@ -189,7 +191,7 @@
     rows, cols, partial, meta, target_copy, sides_copy,
     positions, slab, inv_factor, solved, picked, sides, table, local_sem,
     z1, z1_in, mate1, mate1_in, z2, z2_in, mate2, mate2_in,
-    swap, swap_in, hand, hand_in, plane1, plane1_in, plane2, plane2_in,
+    swap, swap_in, climb, climb_in, hand, hand_in, plane1, plane1_in, plane2, plane2_in,
 ):
     row = lax.axis_index("row")
     col = lax.axis_index("col")
@@ -242,7 +244,6 @@
     ]
 
     slabs.begin()
-    side_parts.begin()
     late = [load(target, target_copy, 6), load(right_sides, sides_copy, 7)]
     for n, values in enumerate(class_tables(positions[...])):
         meta[n:n + 1, :] = values
@@ -251,50 +252,78 @@
     slabs.collect()
     slabs.end()
 
+    share = slots // 2
+    width = PW // 2
+    mine = pl.ds(pl.multiple_of(k * width, width), width)
+    theirs = pl.ds(pl.multiple_of((1 - k) * width, width), width)
+    here = lax.rem(z, 2) * share
+    above = (row, lax.rem(z + 1, NZ) * 2 + k)
+    below = (row, lax.rem(z + NZ - 1, NZ) * 2 + k)
+
+    def row_piece(slab_index, start, columns):
+        return rows.at[slab_index, pl.ds(start, share), :, columns]
+
+    def send_rows(d, carry):
+        there = lax.rem(row + d, NROW)
+        for j in range(share):
+            picked[d, j] = solved[table[0, there * 16 + here + j], :, mine]
+        remote(picked.at[d], row_piece(row, here, mine), swap.at[d], swap_in.at[d], (there, col)).start()
+        return carry
+
+    def pass_rows(origin):
+        ref = row_piece(origin, here, mine)
+        remote(ref, ref, hand.at[0, origin], hand_in.at[0, origin], mate).start()
+
+        @pl.when(origin < NROW // 2)
+        def _():
+            remote(ref, ref, climb.at[origin], climb_in.at[origin], above).start()
+
+        @pl.when(origin >= NROW // 2)
+        def _():
+            remote(ref, ref, climb.at[origin], climb_in.at[origin], below).start()
+
+    def receive_rows(d, carry):
+        origin = lax.rem(row + NROW - d, NROW)
+        ref = row_piece(origin, here, mine)
+        remote(picked.at[d], ref, swap.at[d], swap_in.at[d], (lax.rem(row + d, NROW), col)).wait()
+        pass_rows(origin)
+        return carry
+
+    def receive_climbed(n, carry):
+        ref = row_piece(n, share - here, mine)
+        remote(ref, ref, climb.at[n], climb_in.at[n], above).wait()
+        remote(ref, ref, hand.at[1, n], hand_in.at[1, n], mate).start()
+        return carry
+
+    def take_over(n, carry):
+        for which, start in ((0, here), (1, share - here)):
+            ref = row_piece(n, start, theirs)
+            remote(ref, ref, hand.at[which, n], hand_in.at[which, n], mate).wait()
+        return carry
+
+    lax.fori_loop(1, NROW, send_rows, 0)
     for slot in range(slots):
         cols[row, slot] = solved[table[0, col * 16 + slot]]
     for plane in planes:
         plane.begin()
-
-    share = slots // 2
-    own_share = pl.ds(k * share, share)
-
-    def send_picked(d, carry):
-        there = lax.rem(row + d, NROW)
-        for j in range(share):
-            picked[d, j] = solved[table[0, there * 16 + k * share + j]]
-        remote(picked.at[d], rows.at[row, own_share], swap.at[d], swap_in.at[d], (there, col)).start()
-        return carry
-
-    lax.fori_loop(1, NROW, send_picked, 0)
     for j in range(share):
-        rows[row, k * share + j] = solved[table[0, row * 16 + k * share + j]]
-
-    def hand_over(origin, d):
-        ref = rows.at[origin, own_share]
-        remote(ref, ref, hand.at[d], hand_in.at[d], mate).start()
-
-    def receive_picked(d, carry):
-        origin = lax.rem(row + NROW - d, NROW)
-        ref = rows.at[origin, own_share]
-        remote(picked.at[d], ref, swap.at[d], swap_in.at[d], (lax.rem(row + d, NROW), col)).wait()
-        hand_over(origin, d)
-        return carry
-
-    hand_over(row, 0)
+        rows[row, here + j, :, mine] = solved[table[0, row * 16 + here + j], :, mine]
+    pass_rows(row)
+    side_parts.begin()
     for plane in planes:
         plane.near(0)
         plane.near(1)
-    side_parts.collect()
+    lax.fori_loop(1, NROW, receive_rows, 0)
     for plane in planes:
         plane.across_near(0)
     for plane in planes:
         plane.far(0)
         plane.far(1)
+    side_parts.collect()
     for plane in planes:
         plane.across_near(1)
         plane.across_near(2)
-    lax.fori_loop(1, NROW, receive_picked, 0)
+    lax.fori_loop(0, NROW, receive_climbed, 0)
     for plane in planes:
         plane.across_near(3)
         plane.across_near(4)
@@ -304,13 +333,6 @@
             inv_factor[q], sides[:, q].reshape(PW, NRHS), preferred_element_type=jnp.float32
         )
         partial[q] = value.astype(jnp.bfloat16)
-
-    def take_over(d, carry):
-        origin = lax.rem(row + NROW - d, NROW)
-        ref = rows.at[origin, pl.ds((1 - k) * share, share)]
-        remote(ref, ref, hand.at[d], hand_in.at[d], mate).wait()
-        return carry
-
     lax.fori_loop(0, NROW, take_over, 0)
     for item in range(5):
         for plane in planes:
@@ -341,13 +363,13 @@
             pltpu.VMEM((2, 2, SLAB, PW), jnp.bfloat16),
             pltpu.VMEM((2, PW, PW), jnp.bfloat16),
             pltpu.VMEM((ZERO_BLOCK + 1, SLAB, PW), jnp.bfloat16),
-            pltpu.VMEM((NROW, slots // 2, SLAB, PW), jnp.bfloat16),
+            pltpu.VMEM((NROW, slots // 2, SLAB, PW // 2), jnp.bfloat16),
             pltpu.VMEM((NCOL,) + rhs.shape, jnp.bfloat16),
             pltpu.SMEM((8, 256), jnp.int32),
             dma((10,)),
             dma((8,)), dma((8,)), dma((8,)), dma((8,)),
             dma((8,)), dma((8,)), dma((8,)), dma((8,)),
-            dma((16,)), dma((16,)), dma((16,)), dma((16,)),
+            dma((16,)), dma((16,)), dma((16,)), dma((16,)), dma((2, 16)), dma((2, 16)),
             dma((2, 2, 2)), dma((2, 2, 2)), dma((2, 5, 2, 2)), dma((2, 5, 2, 2)),
         ],
         compiler_params=pltpu.CompilerParams(
@@ -395,48 +417,52 @@
             tiles[t] = target[t]
 
     for i in range(slots):
-        @pl.when(i < ((rows_here + 1) // 2) * 2)
+        @pl.when(i < rows_here)
         def _():
             left[i * TILE:(i + 1) * TILE, :] = rows[:, i].reshape(TILE, PW)
 
-        @pl.when(i < ((cols_here + 1) // 2) * 2)
+        @pl.when(i < cols_here)
         def _():
             right[i * TILE:(i + 1) * TILE, :] = cols[:, i].reshape(TILE, PW)
 
     sides[...] = right_sides[...]
 
     half = slots // 2
-
-    def column_pair(jp, carry):
-        factor = right[pl.ds(pl.multiple_of(jp * 256, 256), 256), :]
-        for part in range(2):
-            @pl.when(part * half < rows_here)
-            def _():
+    row_split, col_split = meta[4, row], meta[4, col]
+
+    for q in range(2):
+        row_from, row_to = (0, row_split) if q == 0 else (row_split, rows_here)
+        col_from, col_to = (0, col_split) if q == 0 else (col_split, cols_here)
+
+        def column_pair(jp, carry):
+            j = col_from + jp * 2
+            factor = right[pl.ds(pl.multiple_of(j * TILE, TILE), 2 * TILE), :]
+
+            def row_group(part, carry):
+                start = row_from + part * half
                 product[...] = lax.dot_general(
-                    left[part * half * TILE:(part + 1) * half * TILE, :],
+                    left[pl.ds(pl.multiple_of(start * TILE, TILE), half * TILE), :],
                     factor,
                     (((1,), (1,)), ((), ())),
                     preferred_element_type=jnp.float32,
                 )
 
                 def subtract(i, carry):
-                    left_at = meta[1, row + part * half + i]
+                    t = meta[1, row + start + i] & 7
                     for b in range(2):
-                        right_at = meta[1, col + jp * 2 + b]
-
-                        @pl.when((jp * 2 + b < cols_here) & ((left_at >> 3) == (right_at >> 3)))
+                        @pl.when(j + b < col_to)
                         def _():
-                            at = (left_at & 7, pl.ds(right_at & 7, TILE, 8), slice(None))
+                            at = (t, pl.ds(meta[1, col + j + b] & 7, TILE, 8), slice(None))
                             block = product[pl.ds(pl.multiple_of(i * TILE, TILE), TILE), b * TILE:(b + 1) * TILE]
                             tiles[at] = tiles[at] - block
 
                     return carry
 
-                lax.fori_loop(0, jnp.minimum(rows_here - part * half, half), subtract, 0)
-
-        return carry
-
-    lax.fori_loop(0, (cols_here + 1) // 2, column_pair, 0)
+                return lax.fori_loop(0, jnp.minimum(row_to - start, half), subtract, carry)
+
+            return lax.fori_loop(0, (row_to - row_from + half - 1) // half, row_group, carry)
+
+        lax.fori_loop(0, (col_to - col_from + 1) // 2, column_pair, 0)
 
     for t in range(count):
         @pl.when(((row_bits >> t) & 1) == 1)
@@ -475,8 +501,8 @@
         scratch_shapes=[
             pltpu.VMEM(target.shape, jnp.float32),
             pltpu.VMEM(right_sides.shape, jnp.float32),
-            pltpu.VMEM((slots * TILE, PW), jnp.bfloat16),
-            pltpu.VMEM((slots * TILE, PW), jnp.bfloat16),
+            pltpu.VMEM(((slots + slots // 2) * TILE, PW), jnp.bfloat16),
+            pltpu.VMEM(((slots + 1) * TILE, PW), jnp.bfloat16),
             pltpu.VMEM((slots // 2 * TILE, 2 * TILE), jnp.float32),
             pltpu.SemaphoreType.DMA((8,)),
             pltpu.SemaphoreType.DMA,

time: 51.6 us -> 46.6 us (0.903)
  Pallas kernels: 49.7 us -> 44.3 us
    pallas_call x1, Pallas kernels: 43 us -> 39 us  [gather(): pl.pallas_call(functools.partial(gather_kernel, slots), out_shape=(jax.Sh...]
    pallas_call x1, Pallas kernels: 6.63 us -> 5.34 us  [update(): pl.pallas_call(functools.partial(update_kernel, slots), out_shape=(jax.Sh...]
where the time goes in v4:
time: 46.6 us; the launch traced here: 46.1 us
  Pallas kernels  44.3 us (95%)
  between operations  1.29 us (3%)
  local copies, waits for them, and re-layouts  0.51 us (1%)
    pallas_call x1, Pallas kernels, gather(): pl.pallas_call(functools.partial(gather_kernel, slots), out_shape=(jax.Sh...  39 us
    pallas_call x1, Pallas kernels, update(): pl.pallas_call(functools.partial(update_kernel, slots), out_shape=(jax.Sh...  5.34 us

profile of v4, /device:TPU:1, one launch (start us, length us, event | category | flops | bytes accessed | tf_op | source)
XLA Modules:
  0.0 46.1 jit_solution(14705870436064071918)
XLA Ops:
  0.6 39.0 %gather_blocks.3 = (bf16[16,10,8,512]{3,2,1,0:T(8,128)(2,1)S(1)}, bf16[16,10,8,512]{3,2,1,0:T(8,128)(2,1)S(1)}, bf16[2,512,256]{2,1,0:T(8,128)(2,1)S(1)}, s32[8,...) custom-call(s32[2,32]{1,0:T(2,128)} %positions_hbm.1, bf16[2,2,128,512]{3,2,1,0:T(8,128)(2,1)} %panel.1, ...), custom_call_target="tpu_custom_call" | custom-call | tf_op jit(solution)/shard_map/gather_blocks/pallas_call | solution.py:349
  39.6 0.5 %slice.3 = s32[1,1]{1,0:T(1,128)} slice(s32[8,256]{1,0:T(8,128)S(1)} %get-tuple-element.60), slice={[3:4], [0:1]} | slice | bytes 8 | tf_op jit(solution)/shard_map/slice | solution.py:527
  40.8 5.4 %conditional.1 = ((f32[8,1024,128]{2,1,0:T(8,128)}, f32[8,128,256]{2,1,0:T(8,128)})) conditional(s32[]{:T(128)} %bitcast.2, (s32[2,32]{1,0:T(2,128)}, bf16[2,2,128,512]{3,2,1,0:T(8,128)(2,1)}, bf16[2,512,512]{2,1,0:T(8,128)(2,1)}, bf16[2,32,256]{2,1,0:T(8,128)(2,1)}, f32[8,1024,128]{2,1,0:T(8,128)}, /*index=5*/f32[8,128,256]{2,1,0:T(8,128)}) %tuple.29, ...), branch_computations={%region_0.0_spmd, %region_1.0_spmd} | conditional | bytes 8 | solution.py:527
  40.8 5.3 %update_blocks.3 = (f32[8,1024,128]{2,1,0:T(8,128)}, f32[8,128,256]{2,1,0:T(8,128)}) custom-call(s32[8,256]{1,0:T(8,128)S(1)} %get-tuple-element.44.meta, bf16[16,10,8,512]{3,2,1,0:T(8,128)(2,1)S(1)} %get-tuple-element.45.rows, bf16[16,10,8,512]{3,2,1,0:T(8,128)(2,1)S(1)} %get-tuple-element.46.cols, bf16[2,512,256]{2,1,0:T(8,128)(2,1)S(1)} %get-tuple-element.47.partial, ...), custom_call_target="tpu_custom_call" | custom-call | tf_op jit(solution)/shard_map/cond/branch_1_fun/update_blocks/pallas_call | solution.py:493

commit v5 on v4

--- a/solution.py
+++ b/solution.py
@@ -39,6 +39,7 @@
     def finish(self):
         for copy in self.sent:
             copy.wait_send()
+        self.sent = []
 
 
 class ZGather:
@@ -75,86 +76,34 @@
         self.copies, self.cols, self.half = copies, cols, half
         self.x, self.y, self.col = place
         self.send1, self.recv1, self.send2, self.recv2 = send1, recv1, send2, recv2
-        count = cols.shape[1] // 2
-        self.count, self.lead = count, (count + 1) // 2
-
-    def row(self, along, across):
-        dx, dy = (along, across) if self.half == 0 else (across, along)
-        return lax.rem(self.x + dx + NX, NX) * NY + lax.rem(self.y + dy + NY, NY)
-
-    def device(self, along, across):
-        return (self.row(along, across), self.col)
-
-    def ref(self, along, across, part):
-        start = self.half * self.count + (self.lead if part == 1 else 0)
-        size = {None: self.count, 0: self.lead, 1: self.count - self.lead}[part]
-        return self.cols.at[self.row(along, across), pl.ds(start, size)]
-
-    def shift(self, item):
-        return (0, -1, 1, 2, 2)[item]
-
-    def part(self, item):
-        return (None, None, None, 0, 1)[item]
-
-    def across_send(self, item):
-        for way in range(2):
-            self.copies.start(
-                self.ref(self.shift(item), 0, self.part(item)),
-                self.send2.at[item, way, 0],
-                self.recv2.at[item, way, 0],
-                self.device(0, 1 if way == 0 else -1),
-            )
-
-    def begin(self):
-        for way in range(2):
-            self.copies.start(
-                self.ref(0, 0, None), self.send1.at[way, 0], self.recv1.at[way, 0], self.device(1 if way == 0 else -1, 0)
-            )
-        self.across_send(0)
-
-    def near(self, way):
-        towards = 1 if way == 0 else -1
-        self.copies.arrived(
-            self.ref(-towards, 0, None), self.send1.at[way, 0], self.recv1.at[way, 0], self.device(towards, 0)
-        )
-        self.copies.start(
-            self.ref(-towards, 0, way), self.send1.at[way, 1], self.recv1.at[way, 1], self.device(towards, 0)
-        )
-        self.across_send(1 + way)
-
-    def far(self, way):
-        towards = 1 if way == 0 else -1
-        self.copies.arrived(
-            self.ref(2, 0, way), self.send1.at[way, 1], self.recv1.at[way, 1], self.device(towards, 0)
-        )
-        self.across_send(3 + way)
-
-    def across_near(self, item):
-        for way in range(2):
-            towards = 1 if way == 0 else -1
-            self.copies.arrived(
-                self.ref(self.shift(item), -towards, self.part(item)),
-                self.send2.at[item, way, 0],
-                self.recv2.at[item, way, 0],
-                self.device(0, towards),
-            )
-            if item < 3 or item - 3 == way:
-                self.copies.start(
-                    self.ref(self.shift(item), -towards, way),
-                    self.send2.at[item, way, 1],
-                    self.recv2.at[item, way, 1],
-                    self.device(0, towards),
-                )
-
-    def across_far(self, item):
-        for way in range(2):
-            if item < 3 or item - 3 == way:
-                self.copies.arrived(
-                    self.ref(self.shift(item), 2, way),
-                    self.send2.at[item, way, 1],
-                    self.recv2.at[item, way, 1],
-                    self.device(0, 1 if way == 0 else -1),
-                )
+        count = cols.shape[2] // 2
+        self.slots = pl.ds(half * count, count)
+
+    def move(self, stage, distance):
+        along_x = (stage == 1) == (self.half == 0)
+        x = lax.rem(self.x + distance + NX, NX) if along_x else self.x
+        y = self.y if along_x else lax.rem(self.y + distance + NY, NY)
+        return x, y
+
+    def device(self, stage, distance):
+        x, y = self.move(stage, distance)
+        return (x * NY + y, self.col)
+
+    def ref(self, stage, distance):
+        x, y = self.move(stage, distance)
+        if stage == 1:
+            return self.cols.at[x, y, self.slots]
+        return self.cols.at[:, y, self.slots] if self.half == 0 else self.cols.at[x, :, self.slots]
+
+    def send(self, stage):
+        sems = (self.send1, self.recv1) if stage == 1 else (self.send2, self.recv2)
+        for d in (1, 3, 2):
+            self.copies.start(self.ref(stage, 0), sems[0].at[d], sems[1].at[d], self.device(stage, d))
+
+    def receive(self, stage):
+        sems = (self.send1, self.recv1) if stage == 1 else (self.send2, self.recv2)
+        for d in (1, 3, 2):
+            self.copies.arrived(self.ref(stage, -d), sems[0].at[d], sems[1].at[d], self.device(stage, d))
 
 
 def class_tables(panel_rows):
@@ -189,7 +138,7 @@
     slots,
     positions_hbm, panel, inv_hbm, rhs, target, right_sides,
     rows, cols, partial, meta, target_copy, sides_copy,
-    positions, slab, inv_factor, solved, picked, sides, table, local_sem,
+    positions, slab, inv_factor, solved, picked, sides, table, local_sem, ready,
     z1, z1_in, mate1, mate1_in, z2, z2_in, mate2, mate2_in,
     swap, swap_in, climb, climb_in, hand, hand_in, plane1, plane1_in, plane2, plane2_in,
 ):
@@ -208,11 +157,13 @@
     own_rows = pl.ds(pl.multiple_of(row * SLAB, SLAB), SLAB)
     first = [load(panel.at[q, b, own_rows], slab.at[q, b], 2 * q + b) for q in range(2) for b in range(2)]
     first += [load(inv_hbm, inv_factor, 4)]
-    second = [load(rhs, sides.at[col], 5), load(positions_hbm, positions, 9)]
+    second = [load(rhs, sides.at[k, z], 5), load(positions_hbm, positions, 9)]
 
     barrier = pltpu.get_barrier_semaphore()
     partners = [(row, lax.rem(z + d, NZ) * 2 + k) for d in NEAREST] + [mate]
-    partners += [(lax.rem(row + d, NROW), col) for d in range(1, NROW)]
+    ring_x = [(lax.rem(x + d, NX) * NY + y, col) for d in range(1, NX)]
+    ring_y = [(x * NY + lax.rem(y + d, NY), col) for d in range(1, NY)]
+    partners += ring_x + ring_y
     for partner in partners:
         pl.semaphore_signal(barrier, inc=1, device_id=partner, device_id_type=MESH)
 
@@ -235,7 +186,6 @@
     slabs = ZGather(
         copies, lambda origin: solved.at[pl.ds(origin * 4, 4)], place, z1, z1_in, mate1, mate1_in
     )
-    side_parts = ZGather(copies, lambda origin: sides.at[origin], place, z2, z2_in, mate2, mate2_in)
     planes = [
         PlaneGather(
             copies, cols, half, (x, y, col), plane1.at[half], plane1_in.at[half], plane2.at[half], plane2_in.at[half]
@@ -244,6 +194,8 @@
     ]
 
     slabs.begin()
+    for partner in ring_x:
+        pl.semaphore_signal(ready, inc=1, device_id=partner, device_id_type=MESH)
     late = [load(target, target_copy, 6), load(right_sides, sides_copy, 7)]
     for n, values in enumerate(class_tables(positions[...])):
         meta[n:n + 1, :] = values
@@ -251,6 +203,7 @@
     to_scalars.wait()
     slabs.collect()
     slabs.end()
+    pl.semaphore_wait(ready, len(ring_x))
 
     share = slots // 2
     width = PW // 2
@@ -260,8 +213,8 @@
     above = (row, lax.rem(z + 1, NZ) * 2 + k)
     below = (row, lax.rem(z + NZ - 1, NZ) * 2 + k)
 
-    def row_piece(slab_index, start, columns):
-        return rows.at[slab_index, pl.ds(start, share), :, columns]
+    def row_piece(slabs_from, start, columns):
+        return rows.at[slabs_from, pl.ds(start, share), :, columns]
 
     def send_rows(d, carry):
         there = lax.rem(row + d, NROW)
@@ -270,75 +223,53 @@
         remote(picked.at[d], row_piece(row, here, mine), swap.at[d], swap_in.at[d], (there, col)).start()
         return carry
 
-    def pass_rows(origin):
-        ref = row_piece(origin, here, mine)
-        remote(ref, ref, hand.at[0, origin], hand_in.at[0, origin], mate).start()
-
-        @pl.when(origin < NROW // 2)
-        def _():
-            remote(ref, ref, climb.at[origin], climb_in.at[origin], above).start()
-
-        @pl.when(origin >= NROW // 2)
-        def _():
-            remote(ref, ref, climb.at[origin], climb_in.at[origin], below).start()
+    every = pl.ds(0, NROW)
+    lower, upper = pl.ds(0, NROW // 2), pl.ds(NROW // 2, NROW // 2)
 
     def receive_rows(d, carry):
-        origin = lax.rem(row + NROW - d, NROW)
-        ref = row_piece(origin, here, mine)
+        ref = row_piece(lax.rem(row + NROW - d, NROW), here, mine)
         remote(picked.at[d], ref, swap.at[d], swap_in.at[d], (lax.rem(row + d, NROW), col)).wait()
-        pass_rows(origin)
         return carry
 
-    def receive_climbed(n, carry):
-        ref = row_piece(n, share - here, mine)
-        remote(ref, ref, climb.at[n], climb_in.at[n], above).wait()
-        remote(ref, ref, hand.at[1, n], hand_in.at[1, n], mate).start()
-        return carry
-
-    def take_over(n, carry):
-        for which, start in ((0, here), (1, share - here)):
-            ref = row_piece(n, start, theirs)
-            remote(ref, ref, hand.at[which, n], hand_in.at[which, n], mate).wait()
-        return carry
-
+    for slot in range(slots):
+        cols[x, y, slot] = solved[table[0, col * 16 + slot]]
+    for plane in planes:
+        plane.send(1)
     lax.fori_loop(1, NROW, send_rows, 0)
-    for slot in range(slots):
-        cols[row, slot] = solved[table[0, col * 16 + slot]]
-    for plane in planes:
-        plane.begin()
     for j in range(share):
         rows[row, here + j, :, mine] = solved[table[0, row * 16 + here + j], :, mine]
-    pass_rows(row)
-    side_parts.begin()
+    for d in NEAREST:
+        copies.start(sides.at[k, z], z2.at[d], z2_in.at[d], (row, lax.rem(z + d, NZ) * 2 + k))
     for plane in planes:
-        plane.near(0)
-        plane.near(1)
+        plane.receive(1)
+    copies.finish()
+    for plane in planes:
+        plane.send(2)
     lax.fori_loop(1, NROW, receive_rows, 0)
-    for plane in planes:
-        plane.across_near(0)
-    for plane in planes:
-        plane.far(0)
-        plane.far(1)
-    side_parts.collect()
-    for plane in planes:
-        plane.across_near(1)
-        plane.across_near(2)
-    lax.fori_loop(0, NROW, receive_climbed, 0)
-    for plane in planes:
-        plane.across_near(3)
-        plane.across_near(4)
-    side_parts.end()
+    copies.start(row_piece(lower, here, mine), climb.at[0], climb_in.at[0], above)
+    copies.start(row_piece(upper, here, mine), climb.at[1], climb_in.at[1], below)
+    copies.start(row_piece(every, here, mine), hand.at[2], hand_in.at[2], mate)
+    for d in NEAREST:
+        copies.arrived(
+            sides.at[k, lax.rem(z + NZ - d, NZ)], z2.at[d], z2_in.at[d], (row, lax.rem(z + d, NZ) * 2 + k)
+        )
+    copies.start(sides.at[k], mate2.at[0], mate2_in.at[0], mate)
+    for n, part in enumerate((lower, upper)):
+        ref = row_piece(part, share - here, mine)
+        copies.arrived(ref, climb.at[n], climb_in.at[n], above)
+        copies.start(ref, hand.at[n], hand_in.at[n], mate)
+    copies.arrived(sides.at[1 - k], mate2.at[0], mate2_in.at[0], mate)
     for q in range(2):
-        value = jnp.dot(
-            inv_factor[q], sides[:, q].reshape(PW, NRHS), preferred_element_type=jnp.float32
-        )
+        whole = jnp.concatenate([sides[core, chip, q] for chip in range(NZ) for core in range(2)], axis=0)
+        value = jnp.dot(inv_factor[q], whole, preferred_element_type=jnp.float32)
         partial[q] = value.astype(jnp.bfloat16)
-    lax.fori_loop(0, NROW, take_over, 0)
-    for item in range(5):
-        for plane in planes:
-            plane.across_far(item)
     for copy in late:
         copy.wait()
+    copies.arrived(row_piece(every, here, theirs), hand.at[2], hand_in.at[2], mate)
+    for n, part in enumerate((lower, upper)):
+        copies.arrived(row_piece(part, share - here, theirs), hand.at[n], hand_in.at[n], mate)
+    for plane in planes:
+        plane.receive(2)
     copies.finish()
 
 
@@ -350,7 +281,7 @@
         functools.partial(gather_kernel, slots),
         out_shape=(
             jax.ShapeDtypeStruct((NROW, slots, SLAB, PW), jnp.bfloat16),
-            jax.ShapeDtypeStruct((NROW, slots, SLAB, PW), jnp.bfloat16),
+            jax.ShapeDtypeStruct((NX, NY, slots, SLAB, PW), jnp.bfloat16),
             jax.ShapeDtypeStruct((2, PW, NRHS), jnp.bfloat16),
             jax.ShapeDtypeStruct((8, 256), jnp.int32),
             jax.ShapeDtypeStruct(target.shape, jnp.float32),
@@ -364,13 +295,13 @@
             pltpu.VMEM((2, PW, PW), jnp.bfloat16),
             pltpu.VMEM((ZERO_BLOCK + 1, SLAB, PW), jnp.bfloat16),
             pltpu.VMEM((NROW, slots // 2, SLAB, PW // 2), jnp.bfloat16),
-            pltpu.VMEM((NCOL,) + rhs.shape, jnp.bfloat16),
+            pltpu.VMEM((2, NZ) + rhs.shape, jnp.bfloat16),
             pltpu.SMEM((8, 256), jnp.int32),
-            dma((10,)),
+            dma((10,)), pltpu.SemaphoreType.REGULAR,
             dma((8,)), dma((8,)), dma((8,)), dma((8,)),
-            dma((8,)), dma((8,)), dma((8,)), dma((8,)),
-            dma((16,)), dma((16,)), dma((16,)), dma((16,)), dma((2, 16)), dma((2, 16)),
-            dma((2, 2, 2)), dma((2, 2, 2)), dma((2, 5, 2, 2)), dma((2, 5, 2, 2)),
+            dma((8,)), dma((8,)), dma((1,)), dma((1,)),
+            dma((16,)), dma((16,)), dma((2,)), dma((2,)), dma((3,)), dma((3,)),
+            dma((2, 4)), dma((2, 4)), dma((2, 4)), dma((2, 4)),
         ],
         compiler_params=pltpu.CompilerParams(
             collective_id=number, has_side_effects=True, vmem_limit_bytes=24 << 20
@@ -490,6 +421,7 @@
 def update(slots, meta, rows, cols, partial, target, right_sides):
     vmem = pl.BlockSpec(memory_space=pltpu.VMEM)
     hbm = pl.BlockSpec(memory_space=pltpu.MemorySpace.HBM)
+    cols = cols.reshape(NROW, slots, SLAB, PW)
     return pl.pallas_call(
         functools.partial(update_kernel, slots),
         out_shape=(

time: 46.6 us -> 43 us (0.923)
  Pallas kernels: 44.3 us -> 40.4 us
    pallas_call x1, Pallas kernels: 5.34 us -> 3.34 us  [update(): pl.pallas_call(functools.partial(update_kernel, slots), out_shape=(jax.Sh...]
    pallas_call x1, Pallas kernels: 39 us -> 37.1 us  [gather(): pl.pallas_call(functools.partial(gather_kernel, slots), out_shape=(jax.Sh...]
where the time goes in v5:
time: 43 us; the launch traced here: 42.2 us
  Pallas kernels  40.4 us (94%)
  between operations  1.29 us (3%)
  local copies, waits for them, and re-layouts  0.51 us (1%)
    pallas_call x1, Pallas kernels, gather(): pl.pallas_call(functools.partial(gather_kernel, slots), out_shape=(jax.Sh...  37.1 us
    pallas_call x1, Pallas kernels, update(): pl.pallas_call(functools.partial(update_kernel, slots), out_shape=(jax.Sh...  3.34 us

profile of v5, /device:TPU:1, one launch (start us, length us, event | category | flops | bytes accessed | tf_op | source)
XLA Modules:
  0.0 42.2 jit_solution(18323388419339772961)
XLA Ops:
  0.6 37.1 %gather_blocks.3 = (bf16[16,10,8,512]{3,2,1,0:T(8,128)(2,1)S(1)}, bf16[4,4,10,8,512]{4,3,2,1,0:T(8,128)(2,1)S(1)}, bf16[2,512,256]{2,1,0:T(8,128)(2,1)S(1)}, s32...) custom-call(s32[2,32]{1,0:T(2,128)} %positions_hbm.1, bf16[2,2,128,512]{3,2,1,0:T(8,128)(2,1)} %panel.1, ...), custom_call_target="tpu_custom_call" | custom-call | tf_op jit(solution)/shard_map/gather_blocks/pallas_call | solution.py:280
  37.7 0.5 %slice.3 = s32[1,1]{1,0:T(1,128)} slice(s32[8,256]{1,0:T(8,128)S(1)} %get-tuple-element.60), slice={[3:4], [0:1]} | slice | bytes 8 | tf_op jit(solution)/shard_map/slice | solution.py:459
  38.9 3.4 %conditional.1 = ((f32[8,1024,128]{2,1,0:T(8,128)}, f32[8,128,256]{2,1,0:T(8,128)})) conditional(s32[]{:T(128)} %bitcast.4, (s32[2,32]{1,0:T(2,128)}, bf16[2,2,128,512]{3,2,1,0:T(8,128)(2,1)}, bf16[2,512,512]{2,1,0:T(8,128)(2,1)}, bf16[2,32,256]{2,1,0:T(8,128)(2,1)}, f32[8,1024,128]{2,1,0:T(8,128)}, /*index=5*/f32[8,128,256]{2,1,0:T(8,128)}) %tuple.29, ...), branch_computations={%region_0.0_spmd, %region_1.0_spmd} | conditional | bytes 8 | solution.py:459
  38.9 3.3 %update_blocks.3 = (f32[8,1024,128]{2,1,0:T(8,128)}, f32[8,128,256]{2,1,0:T(8,128)}) custom-call(s32[8,256]{1,0:T(8,128)S(1)} %get-tuple-element.44.meta, bf16[16,10,8,512]{3,2,1,0:T(8,128)(2,1)S(1)} %get-tuple-element.45.rows, bf16[16,10,8,512]{3,2,1,0:T(8,128)(2,1)S(1)} %bitcast.12, bf16[2,512,256]{2,1,0:T(8,128)(2,1)S(1)} %get-tuple-element.47.partial, ...), custom_call_target="tpu_custom_call" | custom-call | tf_op jit(solution)/shard_map/cond/branch_1_fun/update_blocks/pallas_call | solution.py:425
